TPU v7x, 32 devices: a whole 2x2x4 slice. The times are simulated.
32 devices in a mesh: rows: 8 (over y, x, core), seq: 4 (over z).
Axes of the slice: x: 2, y: 2, z: 4, core: 2. Of those that a mesh axis runs over, the one named last changes fastest.
Arguments:
- tokens: bfloat16 [8, 1024, 1024], P('rows', 'seq'), may hold values from -6 to 6
- doc_lengths: int32 [8, 8], P('rows'), may hold values from 1 to 512, 1024 in all within a row
- valid_counts: int32 [8], P('rows'), may hold values from 512 to 1024
- norm_in: bfloat16 [1024], replicated, may hold values from 0.099609375 to 1.8984375
- w_in: bfloat16 [1024, 3072], replicated, may hold values from -0.1875 to 0.1875
- w_conv: bfloat16 [3, 1024], replicated, may hold values from -3 to 3
- w_out: bfloat16 [1024, 1024], replicated, may hold values from -0.1875 to 0.1875
- norm_ffn: bfloat16 [1024], replicated, may hold values from 0.099609375 to 1.8984375
- w_gate: bfloat16 [1024, 4608], replicated, may hold values from -0.1875 to 0.1875
- w_up: bfloat16 [1024, 4608], replicated, may hold values from -0.1875 to 0.1875
- w_down: bfloat16 [4608, 1024], replicated, may hold values from -0.1875 to 0.1875
- cotangent: bfloat16 [8, 1024, 1024], P('rows', 'seq'), may hold values from -6 to 6
Outputs:
- layer_out: bfloat16 [8, 1024, 1024], P('rows', 'seq')
- grad_tokens: bfloat16 [8, 1024, 1024], P('rows', 'seq')
- grad_norm_in: float32 [1024], P(('rows', 'seq'))
- grad_w_in: float32 [1024, 3072], P('rows', 'seq')
- grad_w_conv: float32 [3, 1024], P(None, ('rows', 'seq'))
- grad_w_out: float32 [1024, 1024], P('rows', 'seq')
- grad_norm_ffn: float32 [1024], P(('rows', 'seq'))
- grad_w_gate: float32 [1024, 4608], P('rows', 'seq')
- grad_w_up: float32 [1024, 4608], P('rows', 'seq')
- grad_w_down: float32 [4608, 1024], P('rows', 'seq')
Inputs may be any that keep to these rules, and one draw needn't show every extreme that they name: `doc_lengths`: each row's 8 document lengths sum to 1024; the longest is exactly 512. `valid_counts`: positions at or past a row's count are pads.
All inputs are finite; a program needn't handle non-finite values.
Results may differ from a plain program's by a relative error of at most 0.017.
Values may be sent and summed in bfloat16 or wider, within the bound.
A program may use at most 192 MiB of HBM per device.

v0:
```python
import jax
import jax.numpy as jnp
from jax import lax
from jax.sharding import PartitionSpec as P

EPSILON = 1e-05


def passed_along(value, axis, steps):
    count = lax.axis_size(axis)
    first, last = (max(0, -steps), min(count, count - steps))
    return lax.ppermute(value, axis, [(source, source + steps) for source in range(first, last)])


def rms_scale(values):
    return lax.rsqrt(jnp.mean(values * values, axis=-1, keepdims=True) + EPSILON)


def doc_masks(lengths, positions):
    starts = jnp.cumsum(lengths) - lengths
    within = starts[None, :] <= positions[:, None]
    first = jnp.max(jnp.where(within, starts[None, :], 0), axis=1)
    return [(positions - offset >= first).astype(jnp.float32)[:, None] for offset in range(3)]


def weight_grad(left, right):
    return jnp.einsum("ta,tb->ab", left, right, preferred_element_type=jnp.float32)


def back_product(grad, weight):
    return jnp.einsum("tb,ab->ta", grad, weight, preferred_element_type=jnp.float32)


def local(
    tokens,
    doc_lengths,
    valid_counts,
    norm_in,
    w_in,
    w_conv,
    w_out,
    norm_ffn,
    w_gate,
    w_up,
    w_down,
    cotangent,
):
    inputs = tokens[0].astype(jnp.float32)
    span = inputs.shape[0]
    width = inputs.shape[1]
    start_pos = lax.axis_index("seq") * span
    positions = start_pos + jnp.arange(span + 2, dtype=jnp.int32)
    valid = (positions[:span] < valid_counts[0]).astype(jnp.float32)[:, None]
    same = doc_masks(doc_lengths[0], positions)
    taps = w_conv.astype(jnp.float32)
    gain_in = norm_in.astype(jnp.float32)
    gain_ffn = norm_ffn.astype(jnp.float32)
    scale1 = rms_scale(inputs)
    normed = (inputs * scale1 * gain_in).astype(jnp.bfloat16)
    proj = jnp.dot(normed, w_in, preferred_element_type=jnp.float32)
    gate_b = proj[:, :width]
    gate_c = proj[:, width : 2 * width]
    values = proj[:, 2 * width :]
    mixed_in = (valid * gate_b * values).astype(jnp.bfloat16)
    tail_rows = passed_along(mixed_in[span - 2 :], "seq", 1)
    padded = jnp.concatenate([tail_rows, mixed_in], axis=0).astype(jnp.float32)
    conv = jnp.zeros((span, width), jnp.float32)
    for offset in range(3):
        conv = conv + taps[offset] * same[offset][:span] * padded[2 - offset : 2 - offset + span]
    gated = (valid * gate_c * conv).astype(jnp.bfloat16)
    mixer_out = jnp.dot(gated, w_out, preferred_element_type=jnp.float32)
    resid = inputs + mixer_out
    scale2 = rms_scale(resid)
    normed2 = (resid * scale2 * gain_ffn).astype(jnp.bfloat16)
    gate_act = jnp.dot(normed2, w_gate, preferred_element_type=jnp.float32)
    up_act = jnp.dot(normed2, w_up, preferred_element_type=jnp.float32)
    sigmoid_gate = jax.nn.sigmoid(gate_act)
    silu_gate = gate_act * sigmoid_gate
    hidden = (silu_gate * up_act).astype(jnp.bfloat16)
    ffn_out = jnp.dot(hidden, w_down, preferred_element_type=jnp.float32)
    layer_out = (resid + valid * ffn_out).astype(jnp.bfloat16)
    grad_out = cotangent[0].astype(jnp.float32)
    d_ffn = (valid * grad_out).astype(jnp.bfloat16)
    grad_w_down = weight_grad(hidden, d_ffn)
    d_hidden = back_product(d_ffn, w_down)
    d_gate = (d_hidden * up_act * sigmoid_gate * (1.0 + gate_act * (1.0 - sigmoid_gate))).astype(
        jnp.bfloat16
    )
    d_up = (d_hidden * silu_gate).astype(jnp.bfloat16)
    grad_w_gate = weight_grad(normed2, d_gate)
    grad_w_up = weight_grad(normed2, d_up)
    d_normed2 = back_product(d_gate, w_gate) + back_product(d_up, w_up)
    grad_norm_ffn = jnp.sum(d_normed2 * resid * scale2, axis=0)
    scaled_ffn = gain_ffn * d_normed2
    d_resid = (
        grad_out
        + scale2 * scaled_ffn
        - resid * scale2**3 * jnp.mean(scaled_ffn * resid, axis=-1, keepdims=True)
    )
    d_mixer = d_resid.astype(jnp.bfloat16)
    grad_w_out = weight_grad(gated, d_mixer)
    d_gated = back_product(d_mixer, w_out)
    d_conv = (valid * gate_c * d_gated).astype(jnp.bfloat16)
    d_gate_c = valid * conv * d_gated
    head_rows = passed_along(d_conv[:2], "seq", -1)
    extended = jnp.concatenate([d_conv, head_rows], axis=0).astype(jnp.float32)
    d_mixed = jnp.zeros((span, width), jnp.float32)
    conv_rows = []
    for offset in range(3):
        d_mixed = (
            d_mixed
            + taps[offset] * same[offset][offset : offset + span] * extended[offset : offset + span]
        )
        conv_rows.append(
            jnp.sum(
                extended[:span] * same[offset][:span] * padded[2 - offset : 2 - offset + span],
                axis=0,
            )
        )
    grad_w_conv = jnp.stack(conv_rows, axis=0)
    d_proj = jnp.concatenate(
        [valid * values * d_mixed, d_gate_c, valid * gate_b * d_mixed], axis=1
    ).astype(jnp.bfloat16)
    grad_w_in = weight_grad(normed, d_proj)
    d_normed = back_product(d_proj, w_in)
    grad_norm_in = jnp.sum(d_normed * inputs * scale1, axis=0)
    scaled_in = gain_in * d_normed
    grad_tokens = (
        d_resid
        + scale1 * scaled_in
        - inputs * scale1**3 * jnp.mean(scaled_in * inputs, axis=-1, keepdims=True)
    )
    grad_tokens = grad_tokens.astype(jnp.bfloat16)
    part_gain_in, part_in, part_conv, part_out, part_gate, part_up, part_down, part_gain_ffn = (
        lax.psum_scatter(
            grad_norm_in.astype(jnp.bfloat16), "rows", scatter_dimension=0, tiled=True
        ).astype(jnp.float32),
        lax.psum_scatter(
            grad_w_in.astype(jnp.bfloat16), "rows", scatter_dimension=0, tiled=True
        ).astype(jnp.float32),
        lax.psum_scatter(
            grad_w_conv.astype(jnp.bfloat16), "rows", scatter_dimension=1, tiled=True
        ).astype(jnp.float32),
        lax.psum_scatter(
            grad_w_out.astype(jnp.bfloat16), "rows", scatter_dimension=0, tiled=True
        ).astype(jnp.float32),
        lax.psum_scatter(
            grad_w_gate.astype(jnp.bfloat16), "rows", scatter_dimension=0, tiled=True
        ).astype(jnp.float32),
        lax.psum_scatter(
            grad_w_up.astype(jnp.bfloat16), "rows", scatter_dimension=0, tiled=True
        ).astype(jnp.float32),
        lax.psum_scatter(
            grad_w_down.astype(jnp.bfloat16), "rows", scatter_dimension=0, tiled=True
        ).astype(jnp.float32),
        lax.psum_scatter(
            grad_norm_ffn.astype(jnp.bfloat16), "rows", scatter_dimension=0, tiled=True
        ).astype(jnp.float32),
    )
    sum_gain_in, sum_in, sum_conv, sum_out, sum_gate, sum_up, sum_down, sum_gain_ffn = (
        lax.psum_scatter(
            part_gain_in.astype(jnp.bfloat16), "seq", scatter_dimension=0, tiled=True
        ).astype(jnp.float32),
        lax.psum_scatter(
            part_in.astype(jnp.bfloat16), "seq", scatter_dimension=1, tiled=True
        ).astype(jnp.float32),
        lax.psum_scatter(
            part_conv.astype(jnp.bfloat16), "seq", scatter_dimension=1, tiled=True
        ).astype(jnp.float32),
        lax.psum_scatter(
            part_out.astype(jnp.bfloat16), "seq", scatter_dimension=1, tiled=True
        ).astype(jnp.float32),
        lax.psum_scatter(
            part_gate.astype(jnp.bfloat16), "seq", scatter_dimension=1, tiled=True
        ).astype(jnp.float32),
        lax.psum_scatter(
            part_up.astype(jnp.bfloat16), "seq", scatter_dimension=1, tiled=True
        ).astype(jnp.float32),
        lax.psum_scatter(
            part_down.astype(jnp.bfloat16), "seq", scatter_dimension=1, tiled=True
        ).astype(jnp.float32),
        lax.psum_scatter(
            part_gain_ffn.astype(jnp.bfloat16), "seq", scatter_dimension=0, tiled=True
        ).astype(jnp.float32),
    )
    return (
        layer_out[None],
        grad_tokens[None],
        sum_gain_in,
        sum_in,
        sum_conv,
        sum_out,
        sum_gain_ffn,
        sum_gate,
        sum_up,
        sum_down,
    )


def solution(mesh):
    placed = (
        P("rows", "seq", None),
        P("rows", None),
        P("rows"),
        P(),
        P(),
        P(),
        P(),
        P(),
        P(),
        P(),
        P(),
        P("rows", "seq", None),
    )
    return jax.shard_map(
        local,
        mesh=mesh,
        in_specs=placed,
        out_specs=(
            P("rows", "seq", None),
            P("rows", "seq", None),
            P(("rows", "seq")),
            P("rows", "seq"),
            P(None, ("rows", "seq")),
            P("rows", "seq"),
            P(("rows", "seq")),
            P("rows", "seq"),
            P("rows", "seq"),
            P("rows", "seq"),
        ),
        check_vma=False,
    )
```

profile of v0, /device:TPU:0, one launch (start us, length us, event | category | flops | bytes accessed | tf_op | source)
XLA Modules:
  0.0 626.5 jit_solution(5961709602000606534)
XLA Ops:
  10.0 4.9 fusion.28
  16.7 4.9 collective-permute-start
  26.2 8.9 %fusion.40 = f32[256,4608]{1,0:T(8,128)} fusion(bf16[256,1024]{1,0:T(8,128)(2,1)S(1)} %multiply_convert_fusion.7, bf16[1024,4608]{1,0:T(8,128)(2,1)} %param.20), kind=kOutput, calls=%fused_computation.91 | convolution fusion | flops 2415919104 | bytes 14680064 | tf_op jit(solution)/shard_map/dot_general | solution.py:75
  35.1 4.3 fusion.41
  39.4 14.2 %multiply_convert_fusion = (bf16[256,4608]{1,0:T(8,128)(2,1)}, bf16[256,4608]{1,0:T(8,128)(2,1)}, bf16[256,4608]{1,0:T(8,128)(2,1)}) fusion(f32[256,4608]{1,0:T(8,128)} %fusion.40, f32[256,4608]{1,0:T(8,128)} %fusion.41, bf16[4608,1024]{1,0:T(8,128)(2,1)} %param.22, bf16[1,256,1024]{2,1,0:T(8,128)(2,1)S(1)} %copy-done.14, f32[256]{0:T(256)S(1)} %compare_convert_fusion), kind=kOutput, calls=%fused_computation.4 | convolution fusion | flops 2434400256 | bytes 26477568 | tf_op jit(solution)/shard_map/tb,ab->ta/dot_general | solution.py:31
  53.7 4.4 fusion.42
  58.1 5.5 multiply_reduce_fusion
  80.3 5.6 convolution_convert_fusion.3
  86.9 6.8 %convolution_convert_fusion.2 = bf16[1024,4608]{1,0:T(8,128)(2,1)} fusion(bf16[256,1024]{1,0:T(8,128)(2,1)S(1)} %copy-done.3, bf16[256,4608]{1,0:T(8,128)(2,1)} %get-tuple-element.26), kind=kOutput, calls=%fused_computation.2 | convolution fusion | flops 2420637696 | bytes 12320768 | tf_op jit(solution)/shard_map/ta,tb->ab/dot_general | solution.py:27
  93.8 6.8 %convolution_convert_fusion.1 = bf16[1024,4608]{1,0:T(8,128)(2,1)} fusion(bf16[256,1024]{1,0:T(8,128)(2,1)S(1)} %copy-done.3, bf16[256,4608]{1,0:T(8,128)(2,1)} %get-tuple-element.25), kind=kOutput, calls=%fused_computation.1 | convolution fusion | flops 2420637696 | bytes 12320768 | tf_op jit(solution)/shard_map/ta,tb->ab/dot_general | solution.py:27
  101.6 6.9 %convolution_convert_fusion = bf16[4608,1024]{1,0:T(8,128)(2,1)} fusion(bf16[256,4608]{1,0:T(8,128)(2,1)} %get-tuple-element.27, bf16[1,256,1024]{2,1,0:T(8,128)(2,1)S(1)} %copy-done.15, f32[256]{0:T(256)S(1)} %compare_convert_fusion), kind=kOutput, calls=%fused_computation | convolution fusion | flops 2421424128 | bytes 12321792 | tf_op jit(solution)/shard_map/ta,tb->ab/dot_general | solution.py:27
  110.3 44.8 %reduce-scatter.25.cloned.1.call-done = bf16[128,1024]{1,0:T(8,128)(2,1)} async-done(((bf16[1024,1024]{1,0:T(8,128)(2,1)}), bf16[128,1024]{1,0:T(8,128)(2,1)}) %reduce-scatter.25.cloned.1.call-update) | async-done | bytes 262160 | tf_op jit(solution)/shard_map/reduce_scatter | solution.py:144
  155.2 65.1 %reduce-scatter.21.cloned.1.call-done = bf16[128,3072]{1,0:T(8,128)(2,1)} async-done(((bf16[1024,3072]{1,0:T(8,128)(2,1)}), bf16[128,3072]{1,0:T(8,128)(2,1)}) %reduce-scatter.21.cloned.1.call-update) | async-done | bytes 786448 | tf_op jit(solution)/shard_map/reduce_scatter | solution.py:138
  220.4 80.2 %reduce-scatter.29.cloned.1.call-done = bf16[128,4608]{1,0:T(8,128)(2,1)} async-done(((bf16[1024,4608]{1,0:T(8,128)(2,1)}), bf16[128,4608]{1,0:T(8,128)(2,1)}) %reduce-scatter.29.cloned.1.call-update) | async-done | bytes 1179664 | tf_op jit(solution)/shard_map/reduce_scatter | solution.py:147
  303.0 77.8 %reduce-scatter.31.cloned.1.call-done = bf16[128,4608]{1,0:T(8,128)(2,1)} async-done(((bf16[1024,4608]{1,0:T(8,128)(2,1)}), bf16[128,4608]{1,0:T(8,128)(2,1)}) %reduce-scatter.31.cloned.1.call-update) | async-done | bytes 1179664 | tf_op jit(solution)/shard_map/reduce_scatter | solution.py:150
  383.6 77.6 %reduce-scatter.33.cloned.1.call-done = bf16[576,1024]{1,0:T(8,128)(2,1)} async-done(((bf16[4608,1024]{1,0:T(8,128)(2,1)}), bf16[576,1024]{1,0:T(8,128)(2,1)}) %reduce-scatter.33.cloned.1.call-update) | async-done | bytes 1179664 | tf_op jit(solution)/shard_map/reduce_scatter | solution.py:153
  463.7 7.9 %fusion.3 = bf16[1,256,1024]{2,1,0:T(8,128)(2,1)} fusion(f32[256,1024]{1,0:T(8,128)S(1)} %copy-done.7, bf16[256,4608]{1,0:T(8,128)(2,1)} %get-tuple-element.27, bf16[4608,1024]{1,0:T(8,128)(2,1)} %param.22, f32[256]{0:T(256)S(1)} %compare_convert_fusion), kind=kOutput, calls=%fused_computation.25 | convolution fusion | flops 2416705536 | bytes 13370368 | tf_op jit(solution)/shard_map/dot_general | solution.py:80
  471.6 5.7 fusion.18
  477.4 13.0 %all-reduce.4 = (bf16[1024]{0:T(1024)(128)(2,1)S(1)}, bf16[1024]{0:T(1024)(128)(2,1)S(1)}) all-reduce(bf16[1024]{0:T(1024)(128)(2,1)S(1)} %get-tuple-element.15, bf16[1024]{0:T(1024)(128)(2,1)S(1)} %get-tuple-element.13), channel_id=2, replica_groups=mesh['rows'=8,'seq'=4] {'rows'}, use_global_device_ids=true, to_apply=%region_7.8.clone | all-reduce | flops 2048 | bytes 8192
  490.5 11.4 %all-reduce.5 = (bf16[128]{0:T(256)(128)(2,1)S(1)}, bf16[128]{0:T(256)(128)(2,1)S(1)}) all-reduce(bf16[128]{0:T(256)(128)(2,1)S(1)} %dynamic-slice.1, bf16[128]{0:T(256)(128)(2,1)S(1)} %dynamic-slice.5), channel_id=3, replica_groups=mesh['rows'=8,'seq'=4] {'seq'}, use_global_device_ids=true, to_apply=%region_8.9.clone | all-reduce | flops 256 | bytes 1024
  508.6 18.0 %reduce-scatter.23.cloned.1.call-done = bf16[128,768]{1,0:T(8,128)(2,1)} async-done(((bf16[128,3072]{1,0:T(8,128)(2,1)}), bf16[128,768]{1,0:T(8,128)(2,1)}) %reduce-scatter.23.cloned.1.call-update) | async-done | bytes 196624 | tf_op jit(solution)/shard_map/reduce_scatter | solution.py:164
  528.3 29.0 %reduce-scatter.41.cloned.1.call-done = bf16[1152,128]{1,0:T(8,128)(2,1)} async-done(((bf16[4608,128]{1,0:T(8,128)(2,1)}), bf16[1152,128]{1,0:T(8,128)(2,1)}) %reduce-scatter.41.cloned.1.call-update) | async-done | bytes 294928
  559.3 28.3 %reduce-scatter.43.cloned.1.call-done = bf16[1152,128]{1,0:T(8,128)(2,1)} async-done(((bf16[4608,128]{1,0:T(8,128)(2,1)}), bf16[1152,128]{1,0:T(8,128)(2,1)}) %reduce-scatter.43.cloned.1.call-update) | async-done | bytes 294928
  589.6 28.2 %reduce-scatter.35.cloned.1.call-done = bf16[576,256]{1,0:T(8,128)(2,1)} async-done(((bf16[576,1024]{1,0:T(8,128)(2,1)}), bf16[576,256]{1,0:T(8,128)(2,1)}) %reduce-scatter.35.cloned.1.call-update) | async-done | bytes 294928 | tf_op jit(solution)/shard_map/reduce_scatter | solution.py:179
  (149 shorter events, 49.5 us)
Async XLA Ops:
  7.2 18.0 %copy-start = (bf16[1024,1024]{1,0:T(8,128)(2,1)S(1)}, bf16[1024,1024]{1,0:T(8,128)(2,1)}, u32[]{:S(2)}) copy-start(bf16[1024,1024]{1,0:T(8,128)(2,1)} %param.18) | copy-start | bytes 6291460
  7.2 103.1 %reduce-scatter.37.cloned.1.call-start = ((), (), s32[]{:S(2)}) async-start(), calls=%async_computation.20 | async-start | bytes 294912
  10.0 12.1 %copy-start.22 = (bf16[1024]{0:T(1024)(128)(2,1)S(1)}, bf16[1024]{0:T(1024)(128)(2,1)}, u32[]{:S(2)}) copy-start(bf16[1024]{0:T(1024)(128)(2,1)} %param.19) | copy-start | bytes 6148
  16.7 6.2 collective-permute-start
  26.0 37.7 %copy-start.6 = (f32[256,1024]{1,0:T(8,128)}, f32[256,1024]{1,0:T(8,128)S(1)}, u32[]{:S(2)}) copy-start(f32[256,1024]{1,0:T(8,128)S(1)} %get-tuple-element.47) | copy-start | bytes 3145732
  35.1 18.5 %slice-start = ((s8[9437184]{0:T(1024)(128)(4,1)}), s8[4194304]{0:T(1024)(128)(4,1)S(1)}, s32[]{:S(2)}) async-start(s8[9437184]{0:T(1024)(128)(4,1)} %bitcast.62), calls=%async_computation.24 | async-start | bytes 8388608
  39.4 14.2 %slice-start.1 = ((s8[9437184]{0:T(1024)(128)(4,1)}), s8[4194304]{0:T(1024)(128)(4,1)S(1)}, s32[]{:S(2)}) async-start(s8[9437184]{0:T(1024)(128)(4,1)} %bitcast.62), calls=%async_computation.25 | async-start | bytes 8388608
  39.4 14.2 %slice-start.2 = ((s8[9437184]{0:T(1024)(128)(4,1)}), s8[1048576]{0:T(1024)(128)(4,1)S(1)}, s32[]{:S(2)}) async-start(s8[9437184]{0:T(1024)(128)(4,1)} %bitcast.62), calls=%async_computation.26 | async-start | bytes 2097152
  66.7 5.8 collective-permute-start.1
  75.8 79.3 %reduce-scatter.25.cloned.1.call-start = ((), (), s32[]{:S(2)}) async-start(), calls=%async_computation.14 | async-start | bytes 2359296 | tf_op jit(solution)/shard_map/reduce_scatter | solution.py:144
  78.0 142.3 %reduce-scatter.21.cloned.1.call-start = ((), (), s32[]{:S(2)}) async-start(), calls=%async_computation.12 | async-start | bytes 7077888 | tf_op jit(solution)/shard_map/reduce_scatter | solution.py:138
  85.9 214.7 %reduce-scatter.29.cloned.1.call-start = ((), (), s32[]{:S(2)}) async-start(), calls=%async_computation.16 | async-start | bytes 10616832 | tf_op jit(solution)/shard_map/reduce_scatter | solution.py:147
  93.8 287.1 %reduce-scatter.31.cloned.1.call-start = ((), (), s32[]{:S(2)}) async-start(), calls=%async_computation.17 | async-start | bytes 10616832 | tf_op jit(solution)/shard_map/reduce_scatter | solution.py:150
  100.6 360.5 %reduce-scatter.33.cloned.1.call-start = ((), (), s32[]{:S(2)}) async-start(), calls=%async_computation.18 | async-start | bytes 10616832 | tf_op jit(solution)/shard_map/reduce_scatter | solution.py:153
  108.6 397.1 %reduce-scatter.39.cloned.1.call-start = ((), (), s32[]{:S(2)}) async-start(), calls=%async_computation.21 | async-start | bytes 40960
  110.3 396.8 %reduce-scatter.27.cloned.1.call-start = ((), (), s32[]{:S(2)}) async-start(), calls=%async_computation.15 | async-start | bytes 327680 | tf_op jit(solution)/shard_map/reduce_scatter | solution.py:170
  155.2 371.4 %reduce-scatter.23.cloned.1.call-start = ((), (), s32[]{:S(2)}) async-start(), calls=%async_computation.13 | async-start | bytes 983040 | tf_op jit(solution)/shard_map/reduce_scatter | solution.py:164
  220.3 336.9 %reduce-scatter.41.cloned.1.call-start = ((), (), s32[]{:S(2)}) async-start(), calls=%async_computation.22 | async-start | bytes 1474560
  303.0 158.2 %copy-start.25 = (u32[32]{0:T(128)S(1)}, u32[32]{0:T(128)}, u32[]{:S(2)}) copy-start(u32[32]{0:T(128)} %constant.37) | copy-start | bytes 388
  303.0 158.8 %copy-start.24 = (u32[32]{0:T(128)S(1)}, u32[32]{0:T(128)}, u32[]{:S(2)}) copy-start(u32[32]{0:T(128)} %constant.41) | copy-start | bytes 388
  303.0 160.7 %copy-start.7 = (f32[256,1024]{1,0:T(8,128)S(1)}, f32[256,1024]{1,0:T(8,128)}, u32[]{:S(2)}) copy-start(f32[256,1024]{1,0:T(8,128)} %copy-done.6) | copy-start | bytes 3145732
  303.0 284.6 %reduce-scatter.43.cloned.1.call-start = ((), (), s32[]{:S(2)}) async-start(), calls=%async_computation.23 | async-start | bytes 1474560
  383.3 234.5 %reduce-scatter.35.cloned.1.call-start = ((), (), s32[]{:S(2)}) async-start(), calls=%async_computation.19 | async-start | bytes 1474560 | tf_op jit(solution)/shard_map/reduce_scatter | solution.py:179
  503.1 116.6 %copy-start.1 = (bf16[1024,1024]{1,0:T(8,128)(2,1)S(1)}, bf16[1024,1024]{1,0:T(8,128)(2,1)}, u32[]{:S(2)}) copy-start(bf16[1024,1024]{1,0:T(8,128)(2,1)} %param.18) | copy-start | bytes 6291460
  (22 other events, 125.4 us)
Sparse Core Ops, SparseCore 0:
  76.0 34.2 reduce-scatter.36
  113.9 41.2 reduce-scatter.24
  158.6 61.7 reduce-scatter.20
  224.1 76.4 reduce-scatter.28
  304.3 76.4 reduce-scatter.30
  384.6 76.4 reduce-scatter.32
  463.5 18.9 reduce-scatter.38
  484.7 17.8 reduce-scatter.26
  505.0 21.5 reduce-scatter.22
  528.8 28.4 reduce-scatter.40
  559.7 27.8 reduce-scatter.42
  589.9 27.8 reduce-scatter.34
where the time goes:
time: 627 us
  waiting for transfers between devices  456 us (73%)
  matrix products  85.6 us (14%)
  blocking collectives  24.4 us (4%)
  other arithmetic  21.2 us (3%)
  between operations  16.7 us (3%)
  local copies, waits for them, and re-layouts  15.5 us (2%)
  starting transfers between devices  7.1 us (1%)
    reduce_scatter x1, waiting for transfers between devices, local(): lax.psum_scatter(grad_w_gate.astype(jnp.bfloat16), 'rows', scatter_dimens...  80.2 us
    reduce_scatter x1, waiting for transfers between devices, local(): lax.psum_scatter(grad_w_up.astype(jnp.bfloat16), 'rows', scatter_dimensio...  77.8 us
    reduce_scatter x1, waiting for transfers between devices, local(): lax.psum_scatter(grad_w_down.astype(jnp.bfloat16), 'rows', scatter_dimens...  77.6 us
    reduce_scatter x1, waiting for transfers between devices, local(): lax.psum_scatter(grad_w_in.astype(jnp.bfloat16), 'rows', scatter_dimensio...  65.1 us
    unnamed x16, waiting for transfers between devices  59.2 us
    reduce_scatter x1, waiting for transfers between devices, local(): lax.psum_scatter(grad_w_out.astype(jnp.bfloat16), 'rows', scatter_dimensi...  44.8 us
    dot_general x5, matrix products, back_product(): jnp.einsum('tb,ab->ta', grad, weight, preferred_element_type=jnp.float32)  30.7 us
    reduce_scatter x1, waiting for transfers between devices, local(): lax.psum_scatter(part_down.astype(jnp.bfloat16), 'seq', scatter_dimension...  28.2 us
  transfers between devices with their start and end apart: 14, of which 12 were waited for; matrix products, arithmetic and copies ran while one was open for 10% of the time, Pallas kernels for 0%

commit v1 on v0

--- a/solution.py
+++ b/solution.py
@@ -1,9 +1,17 @@
+import functools
+
 import jax
 import jax.numpy as jnp
+import numpy as np
 from jax import lax
+from jax.experimental import pallas as pl
+from jax.experimental.pallas import tpu as pltpu
 from jax.sharding import PartitionSpec as P
 
 EPSILON = 1e-05
+BF = jnp.bfloat16
+F32 = jnp.float32
+MESH = pl.DeviceIdType.MESH
 
 
 def passed_along(value, axis, steps):
@@ -31,7 +39,13 @@
     return jnp.einsum("tb,ab->ta", grad, weight, preferred_element_type=jnp.float32)
 
 
-def local(
+def scattered(value, row_dim, seq_dim):
+    part = lax.psum_scatter(value.astype(BF), "rows", scatter_dimension=row_dim, tiled=True)
+    part = lax.psum_scatter(part, "seq", scatter_dimension=seq_dim, tiled=True)
+    return part.astype(F32)
+
+
+def plain(
     tokens,
     doc_lengths,
     valid_counts,
@@ -131,69 +145,954 @@
         - inputs * scale1**3 * jnp.mean(scaled_in * inputs, axis=-1, keepdims=True)
     )
     grad_tokens = grad_tokens.astype(jnp.bfloat16)
-    part_gain_in, part_in, part_conv, part_out, part_gate, part_up, part_down, part_gain_ffn = (
-        lax.psum_scatter(
-            grad_norm_in.astype(jnp.bfloat16), "rows", scatter_dimension=0, tiled=True
-        ).astype(jnp.float32),
-        lax.psum_scatter(
-            grad_w_in.astype(jnp.bfloat16), "rows", scatter_dimension=0, tiled=True
-        ).astype(jnp.float32),
-        lax.psum_scatter(
-            grad_w_conv.astype(jnp.bfloat16), "rows", scatter_dimension=1, tiled=True
-        ).astype(jnp.float32),
-        lax.psum_scatter(
-            grad_w_out.astype(jnp.bfloat16), "rows", scatter_dimension=0, tiled=True
-        ).astype(jnp.float32),
-        lax.psum_scatter(
-            grad_w_gate.astype(jnp.bfloat16), "rows", scatter_dimension=0, tiled=True
-        ).astype(jnp.float32),
-        lax.psum_scatter(
-            grad_w_up.astype(jnp.bfloat16), "rows", scatter_dimension=0, tiled=True
-        ).astype(jnp.float32),
-        lax.psum_scatter(
-            grad_w_down.astype(jnp.bfloat16), "rows", scatter_dimension=0, tiled=True
-        ).astype(jnp.float32),
-        lax.psum_scatter(
-            grad_norm_ffn.astype(jnp.bfloat16), "rows", scatter_dimension=0, tiled=True
-        ).astype(jnp.float32),
-    )
-    sum_gain_in, sum_in, sum_conv, sum_out, sum_gate, sum_up, sum_down, sum_gain_ffn = (
-        lax.psum_scatter(
-            part_gain_in.astype(jnp.bfloat16), "seq", scatter_dimension=0, tiled=True
-        ).astype(jnp.float32),
-        lax.psum_scatter(
-            part_in.astype(jnp.bfloat16), "seq", scatter_dimension=1, tiled=True
-        ).astype(jnp.float32),
-        lax.psum_scatter(
-            part_conv.astype(jnp.bfloat16), "seq", scatter_dimension=1, tiled=True
-        ).astype(jnp.float32),
-        lax.psum_scatter(
-            part_out.astype(jnp.bfloat16), "seq", scatter_dimension=1, tiled=True
-        ).astype(jnp.float32),
-        lax.psum_scatter(
-            part_gate.astype(jnp.bfloat16), "seq", scatter_dimension=1, tiled=True
-        ).astype(jnp.float32),
-        lax.psum_scatter(
-            part_up.astype(jnp.bfloat16), "seq", scatter_dimension=1, tiled=True
-        ).astype(jnp.float32),
-        lax.psum_scatter(
-            part_down.astype(jnp.bfloat16), "seq", scatter_dimension=1, tiled=True
-        ).astype(jnp.float32),
-        lax.psum_scatter(
-            part_gain_ffn.astype(jnp.bfloat16), "seq", scatter_dimension=0, tiled=True
-        ).astype(jnp.float32),
-    )
     return (
         layer_out[None],
         grad_tokens[None],
-        sum_gain_in,
-        sum_in,
-        sum_conv,
-        sum_out,
-        sum_gain_ffn,
-        sum_gate,
-        sum_up,
-        sum_down,
+        scattered(grad_norm_in, 0, 0),
+        scattered(grad_w_in, 0, 1),
+        scattered(grad_w_conv, 1, 1),
+        scattered(grad_w_out, 0, 1),
+        scattered(grad_norm_ffn, 0, 0),
+        scattered(grad_w_gate, 0, 1),
+        scattered(grad_w_up, 0, 1),
+        scattered(grad_w_down, 0, 1),
+    )
+
+
+def dot(a, b):
+    return jnp.dot(a, b, preferred_element_type=F32)
+
+
+def dot_nt(a, b):
+    return lax.dot_general(a, b, (((1,), (1,)), ((), ())), preferred_element_type=F32)
+
+
+def dot_tn(a, b):
+    return lax.dot_general(a, b, (((0,), (0,)), ((), ())), preferred_element_type=F32)
+
+
+def bit_of(value, weight):
+    return lax.rem(lax.div(value, np.int32(weight)), np.int32(2))
+
+
+def flipped(value, weight):
+    return value + weight - 2 * weight * bit_of(value, weight)
+
+
+def loop(count, body):
+    lax.fori_loop(0, count, lambda i, carry: (body(i), carry)[1], 0)
+
+
+def block(index, size):
+    return pl.ds(pl.multiple_of(index * size, size), size)
+
+
+N_SEM = 128
+MASK_VALID, MASK_S0, MASK_S1, MASK_S2, MASK_N1, MASK_N2 = range(6)
+
+
+def scratch_list(span, width, ff, rows, seq):
+    quarter = ff // 4
+    tall = ff // rows
+    slim = width // rows
+    side = width // seq
+    half = slim // 2
+    group = 4 * span
+    return [
+        ("tok", pltpu.VMEM((span, width), BF)),
+        ("cot", pltpu.VMEM((span, width), BF)),
+        ("wout", pltpu.VMEM((width, width), BF)),
+        ("nrm", pltpu.VMEM((2 * span, width), BF)),
+        ("gat", pltpu.VMEM((2 * span, width), BF)),
+        ("dmx", pltpu.VMEM((2 * span, width), BF)),
+        ("dpj", pltpu.VMEM((2 * span, 3 * width), BF)),
+        ("gb", pltpu.VMEM((span, width), BF)),
+        ("va", pltpu.VMEM((span, width), BF)),
+        ("gc", pltpu.VMEM((span, width), F32)),
+        ("mix", pltpu.VMEM((span + 8, width), F32)),
+        ("dc", pltpu.VMEM((span + 8, width), F32)),
+        ("res", pltpu.VMEM((span, width), F32)),
+        ("own", pltpu.VMEM((span, width), F32)),
+        ("loa", pltpu.VMEM((span, width), F32)),
+        ("mask", pltpu.VMEM((span, 128), F32)),
+        ("sc1", pltpu.VMEM((span, 1), F32)),
+        ("sc2", pltpu.VMEM((span, 1), F32)),
+        ("n2", pltpu.VMEM((group, width), BF)),
+        ("df", pltpu.VMEM((group, width), BF)),
+        ("hr", pltpu.VMEM((8, width), F32)),
+        ("hr2", pltpu.VMEM((8, width), F32)),
+        ("ps", pltpu.VMEM((2, span, width), BF)),
+        ("pr", pltpu.VMEM((2, span, width), BF)),
+        ("pz", pltpu.VMEM((span, width), BF)),
+        ("fr", pltpu.VMEM((2, span, width), BF)),
+        ("fz", pltpu.VMEM((span, width), BF)),
+        ("sg", pltpu.VMEM((6, 8, width), F32)),
+        ("sm", pltpu.VMEM((8, 128), F32)),
+        ("gg", pltpu.VMEM((8, slim, quarter), BF)),
+        ("rg1", pltpu.VMEM((4, slim, quarter), BF)),
+        ("rg2", pltpu.VMEM((2, slim, quarter), BF)),
+        ("rg3", pltpu.VMEM((2, slim, quarter), BF)),
+        ("rg4", pltpu.VMEM((slim, quarter), BF)),
+        ("gu", pltpu.VMEM((8, slim, quarter), BF)),
+        ("ru1", pltpu.VMEM((4, slim, quarter), BF)),
+        ("ru2", pltpu.VMEM((2, slim, quarter), BF)),
+        ("ru3", pltpu.VMEM((2, slim, quarter), BF)),
+        ("ru4", pltpu.VMEM((slim, quarter), BF)),
+        ("gd", pltpu.VMEM((8, tall, side), BF)),
+        ("ra1", pltpu.VMEM((2, tall, side), BF)),
+        ("ra2", pltpu.VMEM((2, tall, side), BF)),
+        ("ra3", pltpu.VMEM((tall, side), BF)),
+        ("rb1", pltpu.VMEM((4, tall, side), BF)),
+        ("rb2", pltpu.VMEM((2, tall, side), BF)),
+        ("rb3", pltpu.VMEM((tall, side), BF)),
+        ("rd4", pltpu.VMEM((tall, side), BF)),
+        ("m1", pltpu.VMEM((2, 4, 2, half, width), BF)),
+        ("m2", pltpu.VMEM((2, 4, half, width), BF)),
+        ("m3", pltpu.VMEM((2, 2, half, width), BF)),
+        ("m4", pltpu.VMEM((2, half, width), BF)),
+        ("send", pltpu.SemaphoreType.DMA((N_SEM,))),
+        ("recv", pltpu.SemaphoreType.DMA((N_SEM,))),
+        ("local", pltpu.SemaphoreType.DMA((32,))),
+    ]
+
+
+OPERANDS = [
+    "lengths",
+    "counts",
+    "tokens",
+    "cotangent",
+    "gain1",
+    "taps",
+    "gain2",
+    "w_in",
+    "w_out",
+    "w_gate",
+    "w_up",
+    "w_down",
+    "layer_out",
+    "grad_tokens",
+    "g_in",
+    "g_out",
+    "g_gate",
+    "g_up",
+    "g_down",
+    "small",
+]
+
+
+class Refs:
+    pass
+
+
+class View:
+    def __init__(self, ref, index):
+        self.ref, self.index = ref, index
+
+    def take(self):
+        return self.ref.at[self.index]
+
+
+class At:
+    def __init__(self, ref):
+        self.ref = ref
+
+    def __getitem__(self, index):
+        return View(self.ref, index)
+
+
+def taken(ref):
+    return ref.take() if isinstance(ref, View) else ref
+
+
+def layer_kernel(names, *refs):
+    k = Refs()
+    for name, ref in zip(names, refs):
+        setattr(k, name, ref)
+    span, width = k.tok.shape
+    quarter = k.gg.shape[2]
+    tall, side = k.ra3.shape
+    slim = k.gg.shape[1]
+    half = slim // 2
+    wide = 3 * width // 4
+
+    r = lax.axis_index("rows")
+    s = lax.axis_index("seq")
+    c, x, y = bit_of(r, 1), bit_of(r, 2), bit_of(r, 4)
+    z0, z1 = bit_of(s, 1), bit_of(s, 2)
+    to_c = (flipped(r, 1), s)
+    to_x = (flipped(r, 2), s)
+    to_y = (flipped(r, 4), s)
+    to_z = (r, flipped(s, 1))
+    to_w = (r, flipped(s, 2))
+    to_h = (r, 3 - s)
+    to_t = (flipped(r, 2), flipped(s, 1))
+    to_u = (flipped(flipped(r, 2), 1), flipped(s, 1))
+    partners = (to_c, to_x, to_y, to_z, to_w, to_h, to_t, to_u)
+    after = (r, lax.rem(s + 1, np.int32(4)))
+    before = (r, lax.rem(s + 3, np.int32(4)))
+    first_cols, last_cols = block(1 - z1, width // 2), block(z1, width // 2)
+    active, idle = c == y, c != y
+    holder, lender = c == z1, c != z1
+    not_last, not_first = s < 3, s > 0
+    home = [jnp.logical_and(active, jnp.logical_and(x == z0, y == i)) for i in range(2)]
+    gives = [jnp.logical_and(active, jnp.logical_not(home[i])) for i in range(2)]
+    targets = [(4 * y + 2 * z0 + i, 2 * z1 + x) for i in range(2)]
+    away = jnp.logical_not(jnp.logical_and(active, x == z0))
+    away_at = [jnp.logical_and(away, c == i) for i in range(2)]
+    other_core = 1 - c
+
+    sems = {}
+    pending = []
+
+    def sem_of(name, count=1):
+        if name not in sems:
+            sems[name] = sum(n for _, n in sems.values()), count
+            assert sum(n for _, n in sems.values()) <= N_SEM
+        return sems[name][0]
+
+    def remote(name, src, dst, device, offset=0, count=1):
+        at = sem_of(name, count) + offset
+        return pltpu.make_async_remote_copy(
+            src_ref=taken(src),
+            dst_ref=taken(dst),
+            send_sem=k.send.at[at],
+            recv_sem=k.recv.at[at],
+            device_id=device,
+            device_id_type=MESH,
+        )
+
+    def send(name, src, dst, device, offset=0, count=1):
+        remote(name, src, dst, device, offset, count).start()
+
+    def later(cond, *args):
+        pending.append((cond, args))
+
+    def post(name, src, dst, device, cond=None, offset=0, count=1):
+        def go():
+            send(name, src, dst, device, offset, count)
+
+        if cond is None:
+            go()
+        else:
+            pl.when(cond)(go)
+        later(cond, name, src, dst, device, offset, count)
+
+    def arrived(name, dst, offset=0, count=1):
+        remote(name, dst, dst, to_c, offset, count).wait_recv()
+
+    local_count = [0]
+
+    def fetch(src, dst):
+        copy = pltpu.make_async_copy(src, dst, k.local.at[local_count[0]])
+        local_count[0] += 1
+        copy.start()
+        return copy
+
+    got_tok = fetch(k.tokens.at[0], k.tok)
+    got_cot = fetch(k.cotangent.at[0], k.cot)
+    barrier = pltpu.get_barrier_semaphore()
+    for device in partners:
+        pl.semaphore_signal(barrier, inc=1, device_id=device, device_id_type=MESH)
+    got_wout = fetch(k.w_out, k.wout)
+
+    position = s * span + lax.broadcasted_iota(jnp.int32, (span, 1), 0)
+    starts = [np.int32(0)]
+    for i in range(k.lengths.shape[1] - 1):
+        starts.append(starts[-1] + k.lengths[0, i])
+
+    def first_of(at):
+        first = jnp.zeros_like(at)
+        for start in starts:
+            first = jnp.maximum(first, jnp.where(start <= at, start, 0))
+        return first
+
+    def flag(test):
+        return jnp.where(test, 1.0, 0.0).astype(F32)
+
+    first0, first1, first2 = (first_of(position + i) for i in range(3))
+    columns = [
+        flag(position < k.counts[0]),
+        flag(position >= first0),
+        flag(position - 1 >= first0),
+        flag(position - 2 >= first0),
+        flag(position >= first1),
+        flag(position >= first2),
+    ]
+    lane = lax.broadcasted_iota(jnp.int32, (span, 128), 1)
+    table = jnp.zeros((span, 128), F32)
+    for i, column in enumerate(columns):
+        table = jnp.where(lane == i, column, table)
+    k.mask[...] = table
+
+    def mask(i, rows=slice(None)):
+        return k.mask[rows, i : i + 1]
+
+    step = 64
+    passes = span // step
+
+    def mixer_forward(win):
+        got_win = fetch(k.w_in, win)
+        got_tok.wait()
+
+        @functools.partial(loop, passes)
+        def _(i):
+            rows = block(i, step)
+            t = k.tok[rows, :].astype(F32)
+            scale = lax.rsqrt(jnp.mean(t * t, axis=-1, keepdims=True) + EPSILON)
+            k.sc1[rows, :] = scale
+            k.nrm[rows, :] = (t * scale * k.gain1[...].astype(F32)).astype(BF)
+
+        got_cot.wait()
+
+        @functools.partial(loop, passes)
+        def _(i):
+            rows = block(i, step)
+            k.df[rows, :] = (mask(MASK_VALID, rows) * k.cot[rows, :].astype(F32)).astype(BF)
+
+        pl.semaphore_wait(barrier, len(partners))
+        own = pl.ds(0, span)
+        post("df_c", At(k.df)[own], At(k.df)[pl.ds(span, span)], to_c)
+        post(
+            "df_z0",
+            At(k.df)[own, first_cols],
+            At(k.df)[pl.ds(2 * span, span), first_cols],
+            to_z,
+        )
+        got_win.wait()
+
+        @functools.partial(loop, width // 256)
+        def _(j):
+            n = k.nrm[:span, :]
+            cols = block(j, 256)
+            gb = dot(n, win[:, cols])
+            va = dot(n, win[:, pl.ds(pl.multiple_of(2 * width + j * 256, 256), 256)])
+            k.gb[:, cols] = gb.astype(BF)
+            k.va[:, cols] = va.astype(BF)
+            k.mix[8:, cols] = (mask(MASK_VALID) * gb * va).astype(BF).astype(F32)
+
+        post("halo", At(k.mix)[pl.ds(span, 8)], k.hr, after, cond=not_last)
+
+        @functools.partial(loop, width // 256)
+        def _(j):
+            cols = block(j, 256)
+            c_cols = pl.ds(pl.multiple_of(width + j * 256, 256), 256)
+            k.gc[:, cols] = dot(k.nrm[:span, :], win[:, c_cols])
+
+    pl.run_scoped(mixer_forward, pltpu.VMEM((width, 3 * width), BF))
+
+    @pl.when(s == 0)
+    def _():
+        k.mix[:8, :] = jnp.zeros((8, width), F32)
+
+    @pl.when(s > 0)
+    def _():
+        arrived("halo", k.hr)
+        k.mix[:8, :] = k.hr[...]
+
+    def tap(i, cols):
+        return k.taps[i : i + 1, cols].astype(F32)
+
+    def conv_of(cols):
+        return (
+            tap(0, cols) * mask(MASK_S0) * k.mix[8 : 8 + span, cols]
+            + tap(1, cols) * mask(MASK_S1) * k.mix[7 : 7 + span, cols]
+            + tap(2, cols) * mask(MASK_S2) * k.mix[6 : 6 + span, cols]
+        )
+
+    @functools.partial(loop, width // 256)
+    def _(j):
+        cols = block(j, 256)
+        k.gat[:span, cols] = (mask(MASK_VALID) * k.gc[:, cols] * conv_of(cols)).astype(BF)
+
+    got_wout.wait()
+
+    @functools.partial(loop, width // 256)
+    def _(j):
+        cols = block(j, 256)
+        k.res[:, cols] = k.tok[:, cols].astype(F32) + dot(k.gat[:span, :], k.wout[:, cols])
+
+    @functools.partial(loop, passes)
+    def _(i):
+        rows = block(i, step)
+        v = k.res[rows, :]
+        scale = lax.rsqrt(jnp.mean(v * v, axis=-1, keepdims=True) + EPSILON)
+        k.sc2[rows, :] = scale
+        k.n2[rows, :] = (v * scale * k.gain2[...].astype(F32)).astype(BF)
+
+    part = span // 2
+    for i in range(2):
+        here = pl.ds(i * part, part)
+        post(f"n2_z{i}", At(k.n2)[here], At(k.n2)[pl.ds(2 * span + i * part, part)], to_z)
+    post("n2_c", At(k.n2)[pl.ds(0, span)], At(k.n2)[pl.ds(span, span)], to_c)
+    post(
+        "df_z1",
+        At(k.df)[pl.ds(0, span), last_cols],
+        At(k.df)[pl.ds(2 * span, span), last_cols],
+        to_z,
+    )
+    post("nrm_c", At(k.nrm)[pl.ds(0, span)], At(k.nrm)[pl.ds(span, span)], to_c)
+    post("gat_c", At(k.gat)[pl.ds(0, span)], At(k.gat)[pl.ds(span, span)], to_c)
+
+    q = 2 * c + z0
+
+    def gate_block(first, second, core):
+        return 4 * second_of(second, y) + 2 * second_of(first, x) + core
+
+    def second_of(rel, bit):
+        return rel * bit + (1 - rel) * (1 - bit)
+
+    def feed_forward(wg, wu, wd, hid, dg, du):
+        got_wg = fetch(k.w_gate.at[:, block(q, quarter)], wg)
+        got_wu = fetch(k.w_up.at[:, block(q, quarter)], wu)
+        got_wd = fetch(k.w_down.at[block(q, quarter), :], wd)
+
+        def expand(slot):
+            rows = pl.ds(slot * span, span)
+
+            def tile(cols):
+                n = k.n2[rows, :]
+                g = dot(n, wg[:, cols])
+                u = dot(n, wu[:, cols])
+                sig = jax.nn.sigmoid(g)
+                silu = g * sig
+                hid[rows, cols] = (silu * u).astype(BF)
+                dg[rows, cols] = (u * sig * (1.0 + g * (1.0 - sig))).astype(BF)
+                du[rows, cols] = silu.astype(BF)
+
+            loop(quarter // 256, lambda j: tile(block(j, 256)))
+            if quarter % 256:
+                tile(pl.ds(quarter - quarter % 256, quarter % 256))
+
+        def retreat(slot):
+            rows = pl.ds(slot * span, span)
+
+            def tile(cols):
+                d = dot_nt(k.df[rows, :], wd[cols, :])
+                dg[rows, cols] = (d * dg[rows, cols].astype(F32)).astype(BF)
+                du[rows, cols] = (d * du[rows, cols].astype(F32)).astype(BF)
+
+            loop(quarter // 256, lambda j: tile(block(j, 256)))
+            if quarter % 256:
+                tile(pl.ds(quarter - quarter % 256, quarter % 256))
+
+        def back(slot, store):
+            rows = pl.ds(slot * span, span)
+
+            @functools.partial(loop, width // 256)
+            def _(j):
+                cols = block(j, 256)
+                store(cols, dot_nt(dg[rows, :], wg[cols, :]) + dot_nt(du[rows, :], wu[cols, :]))
+
+        def forth(slot, store):
+            rows = pl.ds(slot * span, span)
+
+            @functools.partial(loop, width // 256)
+            def _(j):
+                cols = block(j, 256)
+                store(cols, dot(hid[rows, :], wd[:, cols]))
+
+        def to_ref(ref, plus=None):
+            def store(cols, value):
+                if plus is not None:
+                    value = value + plus[:, cols].astype(F32)
+                ref[:, cols] = value.astype(ref.dtype)
+
+            return store
+
+        def down_grads(rel_w):
+            for rel_x in range(2):
+                sigma = 2 * second_of(rel_w, z1) + second_of(rel_x, x)
+                value = dot_tn(hid[...], k.df[:, block(sigma, side)])
+                u = 2 * rel_w + rel_x
+                k.gd[u] = value[:tall].astype(BF)
+                k.gd[4 + u] = value[tall:].astype(BF)
+                if rel_x == 0:
+                    post(f"ra1_{rel_w}", At(k.gd)[u], At(k.ra1)[rel_w], to_x)
+                post(f"rb1_{u}", At(k.gd)[4 + u], At(k.rb1)[u], to_y, cond=idle)
+
+        got_wg.wait()
+        got_wu.wait()
+        expand(0)
+        arrived("n2_c", k.n2.at[pl.ds(span, span)])
+        expand(1)
+        got_wd.wait()
+        retreat(0)
+        arrived("df_c", k.df.at[pl.ds(span, span)])
+        retreat(1)
+        back(1, to_ref(k.ps.at[0]))
+        post("pr0", At(k.ps)[0], At(k.pr)[0], to_c)
+        z_rows = pl.ds(2 * span, span)
+        t_rows = pl.ds(3 * span, span)
+        arrived("df_z0", k.df.at[z_rows, first_cols])
+        post("df_t0", At(k.df)[z_rows, first_cols], At(k.df)[t_rows, first_cols], to_c)
+        arrived("pr0", k.pr.at[0])
+        back(0, to_ref(k.own, k.pr.at[0]))
+        for i in range(2):
+            z_part = pl.ds(2 * span + i * part, part)
+            t_part = pl.ds(3 * span + i * part, part)
+            arrived(f"n2_z{i}", k.n2.at[z_part])
+            post(f"n2_t{i}", At(k.n2)[z_part], At(k.n2)[t_part], to_c)
+        expand(2)
+        for i in range(2):
+            arrived(f"n2_t{i}", k.n2.at[pl.ds(3 * span + i * part, part)])
+        expand(3)
+        arrived("df_t0", k.df.at[t_rows, first_cols])
+        down_grads(0)
+        arrived("df_z1", k.df.at[z_rows, last_cols])
+        post("df_t1", At(k.df)[z_rows, last_cols], At(k.df)[t_rows, last_cols], to_c)
+        retreat(2)
+        arrived("df_t1", k.df.at[t_rows, last_cols])
+        retreat(3)
+        down_grads(1)
+        back(3, to_ref(k.ps.at[1]))
+        post("pr1", At(k.ps)[1], At(k.pr)[1], to_c)
+
+        def gate_up(rel):
+            @functools.partial(loop, 4)
+            def _(i):
+                second, core = lax.div(i, np.int32(2)), lax.rem(i, np.int32(2))
+                rho = 4 * second_of(second, y) + 2 * second_of(rel, x) + core
+                k.gg[4 * rel + i] = dot_tn(k.n2[:, block(rho, slim)], dg[...]).astype(BF)
+                if rel == 0:
+                    send("rg1", k.gg.at[i], k.rg1.at[i], to_x, i, 4)
+                rho = 4 * second_of(rel, y) + 2 * second_of(second, x) + core
+                k.gu[4 * rel + i] = dot_tn(k.n2[:, block(rho, slim)], du[...]).astype(BF)
+                if rel == 0:
+                    send("ru1", k.gu.at[i], k.ru1.at[i], to_y, i, 4)
+
+        gate_up(0)
+        for i in range(4):
+            later(None, "rg1", At(k.gg)[i], At(k.rg1)[i], to_x, i, 4)
+            later(None, "ru1", At(k.gu)[i], At(k.ru1)[i], to_y, i, 4)
+        arrived("pr1", k.pr.at[1])
+        back(2, to_ref(k.pr.at[1], k.pr.at[1]))
+        post("pz", At(k.pr)[1], k.pz, to_z)
+        gate_up(1)
+        down_x(0)
+        down_x(1)
+        for i in range(2):
+            cond, args = next(p for p in pending if p[1][0] == f"pr{i}")
+            remote(*args).wait_send()
+            pending.remove((cond, args))
+        forth(1, to_ref(k.ps.at[0]))
+        post("fr0", At(k.ps)[0], At(k.fr)[0], to_c)
+        forth(3, to_ref(k.ps.at[1]))
+        post("fr1", At(k.ps)[1], At(k.fr)[1], to_c)
+        arrived("fr1", k.fr.at[1])
+        forth(2, to_ref(k.fr.at[1], k.fr.at[1]))
+        post("fz", At(k.fr)[1], k.fz, to_z)
+        arrived("fr0", k.fr.at[0])
+
+        def store_out(cols, value):
+            value = value + k.fr[0, :, cols].astype(F32)
+            k.loa[:, cols] = k.res[:, cols] + mask(MASK_VALID) * value
+
+        forth(0, store_out)
+
+    def add(dst, src):
+        dst[...] = (dst[...].astype(F32) + src[...].astype(F32)).astype(BF)
+
+    def down_x(rel_w):
+        arrived(f"ra1_{rel_w}", k.ra1.at[rel_w])
+        add(k.ra1.at[rel_w], k.gd.at[2 * rel_w + 1])
+        post(f"ra2_{rel_w}", At(k.ra1)[rel_w], At(k.ra2)[rel_w], to_y, cond=idle)
+
+    def down_y(rel_w):
+        @pl.when(active)
+        def _():
+            arrived(f"ra2_{rel_w}", k.ra2.at[rel_w])
+            add(k.ra2.at[rel_w], k.ra1.at[rel_w])
+
+        if rel_w == 0:
+            post("ra3", At(k.ra2)[0], k.ra3, to_w, cond=active)
+
+    def up_y(u):
+        @pl.when(active)
+        def _():
+            arrived(f"rb1_{u}", k.rb1.at[u])
+            add(k.rb1.at[u], k.gd.at[4 + u])
+
+        if u % 2 == 0:
+            post(f"rb2_{u // 2}", At(k.rb1)[u], At(k.rb2)[u // 2], to_x, cond=active)
+
+    def up_x(rel_w):
+        @pl.when(active)
+        def _():
+            arrived(f"rb2_{rel_w}", k.rb2.at[rel_w])
+            add(k.rb2.at[rel_w], k.rb1.at[2 * rel_w + 1])
+
+        if rel_w == 0:
+            post("rb3", At(k.rb2)[0], k.rb3, to_w, cond=active)
+
+    stored = []
+
+    def down_last(i):
+        got, mine = (k.ra3, k.ra2.at[1]) if i == 0 else (k.rb3, k.rb2.at[1])
+
+        @pl.when(active)
+        def _():
+            arrived("ra3" if i == 0 else "rb3", got)
+            add(got, mine)
+
+        post(f"rd4_{i}", got, k.rd4, targets[i], cond=gives[i])
+        put(got, k.g_down, home[i])
+
+    def put(src, dst, cond=None):
+        at = local_count[0]
+        local_count[0] += 1
+        copy = pltpu.make_async_copy(src, dst, k.local.at[at])
+        if cond is None:
+            copy.start()
+        else:
+            pl.when(cond)(copy.start)
+        stored.append((cond, copy))
+
+    def down_take():
+        for i in range(2):
+
+            @pl.when(away_at[i])
+            def _():
+                arrived(f"rd4_{i}", k.rd4)
+
+        put(k.rd4, k.g_down, away)
+
+    def wide_1(tag, i):
+        first, own, next_, device = (
+            (k.rg1, k.gg, k.rg2, to_y) if tag == "g" else (k.ru1, k.gu, k.ru2, to_x)
+        )
+        arrived(f"r{tag}1", first.at[i], i, 4)
+        add(first.at[i], own.at[4 + i])
+        if i < 2:
+            post(f"r{tag}2_{i}", At(first)[i], At(next_)[i], device)
+
+    def wide_2(tag, i):
+        first, got, next_ = (k.rg1, k.rg2, k.rg3) if tag == "g" else (k.ru1, k.ru2, k.ru3)
+        arrived(f"r{tag}2_{i}", got.at[i])
+        add(got.at[i], first.at[2 + i])
+        post(f"r{tag}3_{i}", At(got)[i], At(next_)[i], to_w, cond=lender)
+
+    def wide_3(tag):
+        got, mine, last, out = (
+            (k.rg3, k.rg2, k.rg4, k.g_gate) if tag == "g" else (k.ru3, k.ru2, k.ru4, k.g_up)
+        )
+
+        @pl.when(holder)
+        def _():
+            for i in range(2):
+                arrived(f"r{tag}3_{i}", got.at[i])
+                add(got.at[i], mine.at[i])
+
+        post(f"r{tag}4", At(got)[other_core], last, to_c, cond=holder)
+        put(got.at[c], out, holder)
+
+    def wide_4(tag):
+        last, out = (k.rg4, k.g_gate) if tag == "g" else (k.ru4, k.g_up)
+
+        @pl.when(lender)
+        def _():
+            arrived(f"r{tag}4", last)
+
+        put(last, out, lender)
+
+    def mix_1(h, b, w):
+        i = 2 * b + w
+        arrived(f"m1_{h}_{i}", k.m1.at[h, i])
+        add(k.m1.at[h, i], gm_ref.at[h, 1, i])
+        post(f"m2_{h}_{i}", At(k.m1)[h, i, 0], At(k.m2)[h, i], to_z)
+
+    def mix_2(h, b, w):
+        i = 2 * b + w
+        arrived(f"m2_{h}_{i}", k.m2.at[h, i])
+        add(k.m2.at[h, i], k.m1.at[h, i, 1])
+        if w == 0:
+            post(f"m3_{h}_{b}", At(k.m2)[h, i], At(k.m3)[h, b], to_w)
+
+    def mix_3(h, b):
+        arrived(f"m3_{h}_{b}", k.m3.at[h, b])
+        add(k.m3.at[h, b], k.m2.at[h, 2 * b + 1])
+        if b == 0:
+            post(f"m4_{h}", At(k.m3)[h, 0], At(k.m4)[h], to_y if h == 0 else to_x)
+
+    def mix_4(h):
+        arrived(f"m4_{h}", k.m4.at[h])
+        add(k.m4.at[h], k.m3.at[h, 1])
+        rows = pl.ds(h * half, half)
+        put(k.m4.at[h, :, pl.ds(0, wide)], k.g_in.at[rows, :])
+        put(k.m4.at[h, :, pl.ds(wide, width - wide)], k.g_out.at[rows, :])
+
+    small_to = (to_c, to_x, to_y, to_z, to_w)
+
+    def small_send(i):
+        post(f"sg{i}", At(k.sg)[i], At(k.sg)[i + 1], small_to[i])
+
+    def small_take(i):
+        arrived(f"sg{i}", k.sg.at[i + 1])
+        k.sg[i + 1] = k.sg[i + 1] + k.sg[i]
+
+    pl.run_scoped(
+        feed_forward,
+        pltpu.VMEM((width, quarter), BF),
+        pltpu.VMEM((width, quarter), BF),
+        pltpu.VMEM((quarter, width), BF),
+        pltpu.VMEM((4 * span, quarter), BF),
+        pltpu.VMEM((4 * span, quarter), BF),
+        pltpu.VMEM((4 * span, quarter), BF),
+    )
+
+    gm_ref = None
+
+    def mixer_backward(win, gm):
+        nonlocal gm_ref
+        gm_ref = gm
+        got_win = fetch(k.w_in, win)
+        arrived("pz", k.pz)
+        k.sg[0] = jnp.zeros((8, width), F32)
+
+        @functools.partial(loop, passes)
+        def _(i):
+            rows = block(i, step)
+            d = k.own[rows, :] + k.pz[rows, :].astype(F32)
+            v = k.res[rows, :]
+            scale = k.sc2[rows, :]
+            scaled = k.gain2[...].astype(F32) * d
+            k.sg[0, 1:2, :] = k.sg[0, 1:2, :] + jnp.sum(d * v * scale, axis=0, keepdims=True)
+            d = (
+                k.cot[rows, :].astype(F32)
+                + scale * scaled
+                - v * (scale * scale * scale) * jnp.mean(scaled * v, axis=-1, keepdims=True)
+            )
+            k.own[rows, :] = d
+            k.dmx[rows, :] = d.astype(BF)
+
+        post("dmx_c", At(k.dmx)[pl.ds(0, span)], At(k.dmx)[pl.ds(span, span)], to_c)
+
+        @functools.partial(loop, width // 256)
+        def _(j):
+            cols = block(j, 256)
+            d = dot_nt(k.dmx[:span, :], k.wout[cols, :])
+            valid = mask(MASK_VALID)
+            k.dc[:span, cols] = (valid * k.gc[:, cols] * d).astype(BF).astype(F32)
+            c_cols = pl.ds(pl.multiple_of(width + j * 256, 256), 256)
+            k.dpj[:span, c_cols] = (valid * conv_of(cols) * d).astype(BF)
+
+        post("halo2", At(k.dc)[pl.ds(0, 8)], k.hr2, before, cond=not_first)
+
+        @pl.when(s == 3)
+        def _():
+            k.dc[span:, :] = jnp.zeros((8, width), F32)
+
+        @pl.when(s < 3)
+        def _():
+            arrived("halo2", k.hr2)
+            k.dc[span:, :] = k.hr2[...]
+
+        @functools.partial(loop, width // 256)
+        def _(j):
+            cols = block(j, 256)
+            d0 = k.dc[:span, cols]
+            d = (
+                tap(0, cols) * mask(MASK_S0) * d0
+                + tap(1, cols) * mask(MASK_N1) * k.dc[1 : 1 + span, cols]
+                + tap(2, cols) * mask(MASK_N2) * k.dc[2 : 2 + span, cols]
+            )
+            valid = mask(MASK_VALID)
+            k.dpj[:span, cols] = (valid * k.va[:, cols].astype(F32) * d).astype(BF)
+            x_cols = pl.ds(pl.multiple_of(2 * width + j * 256, 256), 256)
+            k.dpj[:span, x_cols] = (valid * k.gb[:, cols].astype(F32) * d).astype(BF)
+            for i, m in ((0, MASK_S0), (1, MASK_S1), (2, MASK_S2)):
+                k.sg[0, 2 + i : 3 + i, cols] = jnp.sum(
+                    d0 * mask(m) * k.mix[8 - i : 8 - i + span, cols], axis=0, keepdims=True
+                )
+
+        post("dpj_c", At(k.dpj)[pl.ds(0, span)], At(k.dpj)[pl.ds(span, span)], to_c)
+        for name, ref in (("nrm_c", k.nrm), ("gat_c", k.gat), ("dmx_c", k.dmx), ("dpj_c", k.dpj)):
+            arrived(name, ref.at[pl.ds(span, span)])
+
+        for rel_x in range(2):
+            for rel_y in range(2):
+                rho = 4 * second_of(rel_y, y) + 2 * second_of(rel_x, x) + c
+
+                @functools.partial(loop, 4)
+                def _(i):
+                    w, j0 = lax.div(i, np.int32(2)), lax.rem(i, np.int32(2))
+                    sigma = 2 * second_of(w, z1) + second_of(j0, z0)
+                    value = dot_tn(k.nrm[:, block(rho, slim)], k.dpj[:, block(sigma, wide)])
+                    lower, upper = 2 * rel_y + w, 2 * rel_x + w
+                    gm[0, rel_x, lower, j0, :, :wide] = value[:half].astype(BF)
+                    gm[1, rel_y, upper, j0, :, :wide] = value[half:].astype(BF)
+                    value = dot_tn(k.gat[:, block(rho, slim)], k.dmx[:, block(sigma, side)])
+                    gm[0, rel_x, lower, j0, :, wide:] = value[:half].astype(BF)
+                    gm[1, rel_y, upper, j0, :, wide:] = value[half:].astype(BF)
+
+                for w in range(2):
+                    if rel_x == 0:
+                        i = 2 * rel_y + w
+                        post(f"m1_0_{i}", At(gm)[0, 0, i], At(k.m1)[0, i], to_x)
+                    if rel_y == 0:
+                        i = 2 * rel_x + w
+                        post(f"m1_1_{i}", At(gm)[1, 0, i], At(k.m1)[1, i], to_y)
+
+        got_win.wait()
+
+        @functools.partial(loop, width // 256)
+        def _(j):
+            cols = block(j, 256)
+            k.gc[:, cols] = dot_nt(k.dpj[:span, :], win[cols, :])
+
+        @functools.partial(loop, passes)
+        def _(i):
+            rows = block(i, step)
+            d = k.gc[rows, :]
+            t = k.tok[rows, :].astype(F32)
+            scale = k.sc1[rows, :]
+            scaled = k.gain1[...].astype(F32) * d
+            k.sg[0, 0:1, :] = k.sg[0, 0:1, :] + jnp.sum(d * t * scale, axis=0, keepdims=True)
+            d = (
+                k.own[rows, :]
+                + scale * scaled
+                - t * (scale * scale * scale) * jnp.mean(scaled * t, axis=-1, keepdims=True)
+            )
+            k.tok[rows, :] = d.astype(BF)
+
+        put(k.tok, k.grad_tokens.at[0])
+        small_send(0)
+
+        for u in range(4):
+            up_y(u)
+        for w in range(2):
+            down_y(w)
+        for i in range(4):
+            wide_1("g", i)
+            wide_1("u", i)
+            if i < 4:
+                small_take(i)
+                small_send(i + 1)
+        small_take(4)
+        k.sm[...] = k.sg[5, :, block(r, 128)]
+        put(k.sm, k.small)
+        arrived("fz", k.fz)
+
+        @functools.partial(loop, passes)
+        def _(i):
+            rows = block(i, step)
+            valid = mask(MASK_VALID, rows)
+            k.cot[rows, :] = (k.loa[rows, :] + valid * k.fz[rows, :].astype(F32)).astype(BF)
+
+        put(k.cot, k.layer_out.at[0])
+        up_x(0)
+        up_x(1)
+        for i in range(2):
+            wide_2("g", i)
+            wide_2("u", i)
+        down_last(0)
+        down_last(1)
+        order = [(0, 0), (0, 1), (1, 0), (1, 1)]
+        for b, w in order:
+            for h in range(2):
+                mix_1(h, b, w)
+        wide_3("g")
+        wide_3("u")
+        for b, w in order:
+            for h in range(2):
+                mix_2(h, b, w)
+        wide_4("g")
+        wide_4("u")
+        down_take()
+        for b in range(2):
+            for h in range(2):
+                mix_3(h, b)
+        for h in range(2):
+            mix_4(h)
+        for cond, args in pending:
+            leave = remote(*args).wait_send
+            if cond is None:
+                leave()
+            else:
+                pl.when(cond)(leave)
+        for cond, copy in stored:
+            if cond is None:
+                copy.wait()
+            else:
+                pl.when(cond)(copy.wait)
+
+    pl.run_scoped(
+        mixer_backward,
+        pltpu.VMEM((width, 3 * width), BF),
+        pltpu.VMEM((2, 2, 4, 2, half, width), BF),
+    )
+
+
+def fused(
+    tokens,
+    doc_lengths,
+    valid_counts,
+    norm_in,
+    w_in,
+    w_conv,
+    w_out,
+    norm_ffn,
+    w_gate,
+    w_up,
+    w_down,
+    cotangent,
+):
+    _, span, width = tokens.shape
+    ff = w_gate.shape[1]
+    rows, seq = lax.axis_size("rows"), lax.axis_size("seq")
+    scratch = scratch_list(span, width, ff, rows, seq)
+    anywhere = pl.BlockSpec(memory_space=pl.ANY)
+    scalars = pl.BlockSpec(memory_space=pltpu.SMEM)
+    vectors = pl.BlockSpec(memory_space=pltpu.VMEM)
+    outs = pl.pallas_call(
+        functools.partial(layer_kernel, OPERANDS + [name for name, _ in scratch]),
+        out_shape=[
+            jax.ShapeDtypeStruct((1, span, width), BF),
+            jax.ShapeDtypeStruct((1, span, width), BF),
+            jax.ShapeDtypeStruct((width // rows, 3 * width // seq), BF),
+            jax.ShapeDtypeStruct((width // rows, width // seq), BF),
+            jax.ShapeDtypeStruct((width // rows, ff // seq), BF),
+            jax.ShapeDtypeStruct((width // rows, ff // seq), BF),
+            jax.ShapeDtypeStruct((ff // rows, width // seq), BF),
+            jax.ShapeDtypeStruct((8, 128), F32),
+        ],
+        in_specs=[scalars] * 2
+        + [anywhere] * 2
+        + [vectors] * 3
+        + [anywhere] * 5,
+        out_specs=[anywhere] * 8,
+        scratch_shapes=[shape for _, shape in scratch],
+        compiler_params=pltpu.CompilerParams(
+            collective_id=0, has_side_effects=True, vmem_limit_bytes=67043328
+        ),
+        name="layer",
+    )(
+        doc_lengths,
+        valid_counts,
+        tokens,
+        cotangent,
+        norm_in[None],
+        w_conv,
+        norm_ffn[None],
+        w_in,
+        w_out,
+        w_gate,
+        w_up,
+        w_down,
+    )
+    layer_out, grad_tokens, g_in, g_out, g_gate, g_up, g_down, small = outs
+    piece = width // (rows * seq)
+    small = lax.dynamic_slice(small, (0, lax.axis_index("seq") * piece), (8, piece))
+    return (
+        layer_out,
+        grad_tokens,
+        small[0],
+        g_in.astype(F32),
+        small[2:5],
+        g_out.astype(F32),
+        small[1],
+        g_gate.astype(F32),
+        g_up.astype(F32),
+        g_down.astype(F32),
     )
 
 
@@ -212,8 +1111,9 @@
         P(),
         P("rows", "seq", None),
     )
+    paired = mesh.shape["rows"] == 8 and mesh.shape["seq"] == 4
     return jax.shard_map(
-        local,
+        fused if paired else plain,
         mesh=mesh,
         in_specs=placed,
         out_specs=(

time: 627 us -> 217 us (0.35)
  waiting for transfers between devices: 456 us -> 0 us
  Pallas kernels: 0 us -> 198 us
  matrix products: 85.6 us -> 0 us
  blocking collectives: 24.4 us -> 0 us
  between operations: 16.7 us -> 1.31 us
  other arithmetic: 21.2 us -> 8.64 us
  local copies, waits for them, and re-layouts: 15.5 us -> 8.15 us
  starting transfers between devices: 7.1 us -> 0 us
    reduce_scatter x8 -> x0, waiting for transfers between devices: 392 us -> none  [the longest x1 80.2 us: local(): lax.psum_scatter(grad_w_gate.astype(jnp.bfloat16), 'rows', scatter_dimens...]
    pallas_call x0 -> x1, Pallas kernels: none -> 198 us  [fused(): pl.pallas_call(functools.partial(layer_kernel, OPERANDS + [name for name,...]
    dot_general x15 -> x0, matrix products: 85.6 us -> none  [the longest x5 30.7 us: back_product(): jnp.einsum('tb,ab->ta', grad, weight, preferred_element_type=jnp.float32)]
    unnamed x16 -> x0, waiting for transfers between devices: 59.2 us -> none
    unnamed x2 -> x0, blocking collectives: 24.4 us -> none
    unnamed x74 -> x2, local copies, waits for them, and re-layouts: 15.4 us -> 3.73 us
    ppermute x2 -> x0, starting transfers between devices: 6.39 us -> none  [passed_along(): lax.ppermute(value, axis, [(source, source + steps) for source in range(f...]
  transfers between devices with their start and end apart: 14 -> 0, of which waited for: 12 -> 0; matrix products, arithmetic and copies ran while one was open for 10% -> 0% of each run, Pallas kernels for 0% -> 0%
where the time goes in v1:
time: 217 us; the launch traced here: 216 us
  Pallas kernels  198 us (91%)
  other arithmetic  8.64 us (4%)
  local copies, waits for them, and re-layouts  8.15 us (4%)
    pallas_call x1, Pallas kernels, fused(): pl.pallas_call(functools.partial(layer_kernel, OPERANDS + [name for name,...  198 us

profile of v1, /device:TPU:0, one launch (start us, length us, event | category | flops | bytes accessed | tf_op | source)
XLA Modules:
  0.0 216.2 jit_solution(4984364406419757224)
XLA Ops:
  0.6 1.3 broadcast_in_dim.6.refs_4_
  1.9 1.3 broadcast_in_dim.7.refs_6_
  3.8 198.1 %layer.1 = (bf16[1,256,1024]{2,1,0:T(8,128)(2,1)}, bf16[1,256,1024]{2,1,0:T(8,128)(2,1)}, bf16[128,768]{1,0:T(8,128)(2,1)}, bf16[128,256]{1,0:T(8,128)(2,1)}, bf...) custom-call(s32[1,8]{1,0:T(1,128)} %refs_0_.1, ...), custom_call_target="tpu_custom_call" | custom-call | tf_op jit(solution)/shard_map/layer/pallas_call | solution.py:1046
  202.0 0.8 constant_dynamic-slice_fusion
  202.7 0.5 slice_bitcast_fusion
  203.3 0.6 slice.10
  203.8 1.8 convert_element_type.17
  205.6 1.8 convert_element_type.18
  207.5 1.8 convert_element_type.19
  209.3 1.7 convert_element_type.15
  211.0 1.5 convert_element_type.16
  212.5 1.9 copy.25
  214.3 1.9 copy.26

commit v2 on v0

--- a/solution.py
+++ b/solution.py
@@ -1,9 +1,17 @@
+import functools
+
 import jax
 import jax.numpy as jnp
+import numpy as np
 from jax import lax
+from jax.experimental import pallas as pl
+from jax.experimental.pallas import tpu as pltpu
 from jax.sharding import PartitionSpec as P
 
 EPSILON = 1e-05
+BF = jnp.bfloat16
+F32 = jnp.float32
+MESH = pl.DeviceIdType.MESH
 
 
 def passed_along(value, axis, steps):
@@ -31,7 +39,13 @@
     return jnp.einsum("tb,ab->ta", grad, weight, preferred_element_type=jnp.float32)
 
 
-def local(
+def scattered(value, row_dim, seq_dim):
+    part = lax.psum_scatter(value.astype(BF), "rows", scatter_dimension=row_dim, tiled=True)
+    part = lax.psum_scatter(part, "seq", scatter_dimension=seq_dim, tiled=True)
+    return part.astype(F32)
+
+
+def plain(
     tokens,
     doc_lengths,
     valid_counts,
@@ -131,69 +145,1081 @@
         - inputs * scale1**3 * jnp.mean(scaled_in * inputs, axis=-1, keepdims=True)
     )
     grad_tokens = grad_tokens.astype(jnp.bfloat16)
-    part_gain_in, part_in, part_conv, part_out, part_gate, part_up, part_down, part_gain_ffn = (
-        lax.psum_scatter(
-            grad_norm_in.astype(jnp.bfloat16), "rows", scatter_dimension=0, tiled=True
-        ).astype(jnp.float32),
-        lax.psum_scatter(
-            grad_w_in.astype(jnp.bfloat16), "rows", scatter_dimension=0, tiled=True
-        ).astype(jnp.float32),
-        lax.psum_scatter(
-            grad_w_conv.astype(jnp.bfloat16), "rows", scatter_dimension=1, tiled=True
-        ).astype(jnp.float32),
-        lax.psum_scatter(
-            grad_w_out.astype(jnp.bfloat16), "rows", scatter_dimension=0, tiled=True
-        ).astype(jnp.float32),
-        lax.psum_scatter(
-            grad_w_gate.astype(jnp.bfloat16), "rows", scatter_dimension=0, tiled=True
-        ).astype(jnp.float32),
-        lax.psum_scatter(
-            grad_w_up.astype(jnp.bfloat16), "rows", scatter_dimension=0, tiled=True
-        ).astype(jnp.float32),
-        lax.psum_scatter(
-            grad_w_down.astype(jnp.bfloat16), "rows", scatter_dimension=0, tiled=True
-        ).astype(jnp.float32),
-        lax.psum_scatter(
-            grad_norm_ffn.astype(jnp.bfloat16), "rows", scatter_dimension=0, tiled=True
-        ).astype(jnp.float32),
-    )
-    sum_gain_in, sum_in, sum_conv, sum_out, sum_gate, sum_up, sum_down, sum_gain_ffn = (
-        lax.psum_scatter(
-            part_gain_in.astype(jnp.bfloat16), "seq", scatter_dimension=0, tiled=True
-        ).astype(jnp.float32),
-        lax.psum_scatter(
-            part_in.astype(jnp.bfloat16), "seq", scatter_dimension=1, tiled=True
-        ).astype(jnp.float32),
-        lax.psum_scatter(
-            part_conv.astype(jnp.bfloat16), "seq", scatter_dimension=1, tiled=True
-        ).astype(jnp.float32),
-        lax.psum_scatter(
-            part_out.astype(jnp.bfloat16), "seq", scatter_dimension=1, tiled=True
-        ).astype(jnp.float32),
-        lax.psum_scatter(
-            part_gate.astype(jnp.bfloat16), "seq", scatter_dimension=1, tiled=True
-        ).astype(jnp.float32),
-        lax.psum_scatter(
-            part_up.astype(jnp.bfloat16), "seq", scatter_dimension=1, tiled=True
-        ).astype(jnp.float32),
-        lax.psum_scatter(
-            part_down.astype(jnp.bfloat16), "seq", scatter_dimension=1, tiled=True
-        ).astype(jnp.float32),
-        lax.psum_scatter(
-            part_gain_ffn.astype(jnp.bfloat16), "seq", scatter_dimension=0, tiled=True
-        ).astype(jnp.float32),
-    )
     return (
         layer_out[None],
         grad_tokens[None],
-        sum_gain_in,
-        sum_in,
-        sum_conv,
-        sum_out,
-        sum_gain_ffn,
-        sum_gate,
-        sum_up,
-        sum_down,
+        scattered(grad_norm_in, 0, 0),
+        scattered(grad_w_in, 0, 1),
+        scattered(grad_w_conv, 1, 1),
+        scattered(grad_w_out, 0, 1),
+        scattered(grad_norm_ffn, 0, 0),
+        scattered(grad_w_gate, 0, 1),
+        scattered(grad_w_up, 0, 1),
+        scattered(grad_w_down, 0, 1),
+    )
+
+
+def dot(a, b):
+    return jnp.dot(a, b, preferred_element_type=F32)
+
+
+def dot_nt(a, b):
+    return lax.dot_general(a, b, (((1,), (1,)), ((), ())), preferred_element_type=F32)
+
+
+def dot_tn(a, b):
+    return lax.dot_general(a, b, (((0,), (0,)), ((), ())), preferred_element_type=F32)
+
+
+def bit_of(value, weight):
+    return lax.rem(lax.div(value, np.int32(weight)), np.int32(2))
+
+
+def flipped(value, weights):
+    for weight in (1, 2, 4):
+        if weights & weight:
+            value = value + weight - 2 * weight * bit_of(value, weight)
+    return value
+
+
+def loop(count, body, unroll=True):
+    lax.fori_loop(0, count, lambda i, carry: (body(i), carry)[1], 0, unroll=unroll)
+
+
+def block(index, size):
+    return pl.ds(pl.multiple_of(index * size, size), size)
+
+
+class Name(str):
+    def __call__(self, *index):
+        return (self,) + index
+
+
+class Names:
+    def __getattr__(self, name):
+        return Name(name)
+
+
+N = Names()
+
+STAGES = {
+    N.A: (N.x, N.y, N.z1),
+    N.B: (N.y, N.z1, N.x),
+    N.g0: (N.y, N.x, N.z1),
+    N.g1: (N.x, N.y, N.z1),
+    N.u0: (N.x, N.y, N.z1),
+    N.u1: (N.x, N.y, N.z1),
+    N.m0: (N.y, N.x, N.z0, N.z1),
+    N.m1: (N.y, N.x, N.z0, N.z1),
+}
+ORDER = [
+    N.ex(0), N.tdf(0), N.re(0), N.ex(1), N.re(1), N.bk(1), N.bk(0), N.tn(0),
+    N.ex(2, 0), N.ex(3, 0), N.tn(1), N.ex(2, 1), N.ex(3, 1), N.dn(0), N.tdf(1), N.re(2),
+    N.re(3), N.dn(1), N.B(0, 0), N.bk(3), N.gg(0, 0), N.uu(0, 0), N.gg(1, 0), N.A(0, 0),
+    N.B(0, 1), N.uu(1, 0), N.bk(2), N.gg(0, 1), N.uu(0, 1), N.gg(1, 1), N.uu(1, 1), N.gg(0, 2),
+    N.uu(0, 2), N.gg(1, 2), N.uu(1, 2), N.gg(0, 3), N.uu(0, 3), N.B(0, 2), N.gg(1, 3), N.uu(1, 3),
+    N.A(0, 1), N.fo(1), N.B(1, 0), N.fo(3), N.fo(2), N.fo(0), N.B(0, 3), N.g0(0, 0),
+    N.u0(0, 0), N.B(1, 1), N.g1(0, 0), N.mb(1), N.mb(2), N.g0(0, 1), N.A(1, 0), N.u1(0, 0),
+    N.mb(3), N.mb(4), N.lo, N.u0(0, 1), N.mg(0, 0), N.mg(0, 1), N.u0(1, 0), N.mg(1, 0),
+    N.A(1, 1), N.mg(1, 1), N.g1(0, 1), N.A(2, 0), N.dl(0), N.g1(1, 0), N.u1(0, 1), N.u0(2, 0),
+    N.m0(0, 0), N.u1(1, 0), N.m1(0, 0), N.B(2, 0), N.dl(1), N.g1(2, 0), N.u1(2, 0), N.w3(N.u),
+    N.m0(0, 1), N.w4(N.u), N.g0(1, 0), N.m1(0, 1), N.sg(0), N.g0(2, 0), N.w3(N.g), N.m0(0, 2),
+    N.w4(N.g), N.dt, N.m1(0, 2), N.m0(0, 3), N.sg(1), N.m1(0, 3), N.m0(0, 4), N.m0(1, 0),
+    N.m1(0, 4), N.m1(1, 0), N.m0(0, 5), N.m0(1, 1), N.m1(0, 5), N.m1(1, 1), N.m0(0, 6), N.m0(1, 2),
+    N.m0(2, 0), N.m1(0, 6), N.m1(1, 2), N.m1(2, 0), N.m0(0, 7), N.m0(1, 3), N.m0(2, 1), N.m0(3, 0),
+    N.m1(0, 7), N.m1(1, 3), N.m1(2, 1), N.m1(3, 0),
+]
+FEED = (N.ex, N.re, N.bk, N.dn, N.gg, N.uu, N.fo)
+MIXED = [N.m0, N.m1]
+DOWN = [N.A, N.B]
+GATE = [N.g0, N.g1]
+UP = [N.u0, N.u1]
+N_SEM = 192
+MASK_VALID, MASK_S0, MASK_S1, MASK_S2, MASK_N1, MASK_N2 = range(6)
+
+
+def scatter_of(tag):
+    return (N.x, N.y, N.z0, N.z1) if tag in MIXED else (N.x, N.z1) if tag in DOWN else (N.x, N.y)
+
+
+def counts_of(tag):
+    counts = [2 ** len(scatter_of(tag))]
+    for dim in STAGES[tag]:
+        counts.append(counts[-1] // 2 if dim in scatter_of(tag) else counts[-1])
+    return counts
+
+
+def unit_index(tag, rel):
+    index = 0
+    for dim in STAGES[tag]:
+        if dim in scatter_of(tag):
+            index = 2 * index + rel[dim]
+    return index
+
+
+def unit_bits(tag, index):
+    dims = [dim for dim in STAGES[tag] if dim in scatter_of(tag)]
+    return {dim: (index >> (len(dims) - 1 - i)) & 1 for i, dim in enumerate(dims)}
+
+
+def unit_shape(tag, width, ff, rows, seq):
+    if tag in DOWN:
+        return ff // rows, width // seq
+    if tag in MIXED:
+        return width // rows // len(MIXED), width
+    return width // rows, ff // 4
+
+
+def scratch_list(span, width, ff, rows, seq):
+    group = 4 * span
+    shapes = dict(
+        tok=pltpu.VMEM((span, width), BF),
+        cot=pltpu.VMEM((span, width), BF),
+        wout=pltpu.VMEM((width, width), BF),
+        nrm=pltpu.VMEM((2 * span, width), BF),
+        gat=pltpu.VMEM((2 * span, width), BF),
+        dmx=pltpu.VMEM((2 * span, width), BF),
+        dpj=pltpu.VMEM((2 * span, 3 * width), BF),
+        gb=pltpu.VMEM((span, width), BF),
+        va=pltpu.VMEM((span, width), BF),
+        gc=pltpu.VMEM((span, width), F32),
+        mix=pltpu.VMEM((span + 8, width), F32),
+        dc=pltpu.VMEM((span + 8, width), F32),
+        res=pltpu.VMEM((span, width), F32),
+        own=pltpu.VMEM((span, width), F32),
+        loa=pltpu.VMEM((span, width), F32),
+        mask=pltpu.VMEM((span, 128), F32),
+        sc1=pltpu.VMEM((span, 1), F32),
+        sc2=pltpu.VMEM((span, 1), F32),
+        n2=pltpu.VMEM((group, width), BF),
+        df=pltpu.VMEM((group, width), BF),
+        hr=pltpu.VMEM((8, width), F32),
+        hr2=pltpu.VMEM((8, width), F32),
+        ps=pltpu.VMEM((2, span, width), BF),
+        pr=pltpu.VMEM((2, span, width), BF),
+        pz=pltpu.VMEM((span, width), BF),
+        fr=pltpu.VMEM((2, span, width), BF),
+        fz=pltpu.VMEM((span, width), BF),
+        sg=pltpu.VMEM((8, width), F32),
+        sa=pltpu.VMEM((rows - 1, 8, width // rows), F32),
+        ss=pltpu.VMEM((8, width // rows), F32),
+        sb=pltpu.VMEM((seq - 1, 8, width // rows), F32),
+        rd4=pltpu.VMEM(unit_shape(N.A, width, ff, rows, seq), BF),
+        rg4=pltpu.VMEM(unit_shape(N.g0, width, ff, rows, seq), BF),
+        ru4=pltpu.VMEM(unit_shape(N.u0, width, ff, rows, seq), BF),
+        send=pltpu.SemaphoreType.DMA((N_SEM,)),
+        recv=pltpu.SemaphoreType.DMA((N_SEM,)),
+        local=pltpu.SemaphoreType.DMA((32,)),
+    )
+    for tag in STAGES:
+        unit = unit_shape(tag, width, ff, rows, seq)
+        counts = counts_of(tag)
+        if tag not in MIXED:
+            shapes[N.own, tag] = pltpu.VMEM((counts[0],) + unit, BF)
+        shapes[N.got, tag] = pltpu.VMEM((sum(counts[1:]),) + unit, BF)
+    return shapes
+
+
+OPERANDS = [
+    N.lengths,
+    N.counts,
+    N.tokens,
+    N.cotangent,
+    N.gain1,
+    N.taps,
+    N.gain2,
+    N.w_in,
+    N.w_out,
+    N.w_gate,
+    N.w_up,
+    N.w_down,
+    N.layer_out,
+    N.grad_tokens,
+    N.g_in,
+    N.g_out,
+    N.g_gate,
+    N.g_up,
+    N.g_down,
+    N.small,
+]
+
+
+class Refs:
+    pass
+
+
+class View:
+    def __init__(self, ref, index):
+        self.ref, self.index = ref, index
+
+    def take(self):
+        return self.ref.at[self.index]
+
+
+class At:
+    def __init__(self, ref):
+        self.ref = ref
+
+    def __getitem__(self, index):
+        return View(self.ref, index)
+
+
+def taken(ref):
+    return ref.take() if isinstance(ref, View) else ref
+
+
+def layer_kernel(names, *refs):
+    k = Refs()
+    travelling = {}
+    for name, ref in zip(names, refs):
+        if isinstance(name, tuple):
+            travelling[name] = ref
+        else:
+            setattr(k, name, ref)
+    span, width = k.tok.shape
+    slim, quarter = k.rg4.shape
+    tall, side = k.rd4.shape
+    wide = 3 * width // 4
+
+    r = lax.axis_index("rows")
+    s = lax.axis_index("seq")
+    c, x, y = bit_of(r, 1), bit_of(r, 2), bit_of(r, 4)
+    z0, z1 = bit_of(s, 1), bit_of(s, 2)
+    row_peers = [flipped(r, i) for i in range(8)]
+    seq_peers = [flipped(s, i) for i in range(4)]
+    to_c = (row_peers[1], s)
+    to_z = (r, seq_peers[1])
+    to_dim = {
+        N.x: (row_peers[2], s),
+        N.y: (row_peers[4], s),
+        N.z0: to_z,
+        N.z1: (r, seq_peers[2]),
+    }
+    partners = [(row, s) for row in row_peers[1:]] + [(r, seq) for seq in seq_peers[1:]]
+    partners += [(row_peers[2], seq_peers[1]), (row_peers[3], seq_peers[1])]
+    after = (r, lax.rem(s + 1, np.int32(4)))
+    before = (r, lax.rem(s + 3, np.int32(4)))
+    first_cols, last_cols = block(1 - z1, width // 2), block(z1, width // 2)
+    active, idle = c == y, c != y
+    holder, lender = c == z1, c != z1
+    not_last, not_first = s < 3, s > 0
+    home = [jnp.logical_and(active, jnp.logical_and(x == z0, y == i)) for i in range(2)]
+    gives = [jnp.logical_and(active, jnp.logical_not(home[i])) for i in range(2)]
+    targets = [(4 * y + 2 * z0 + i, 2 * z1 + x) for i in range(2)]
+    away = jnp.logical_not(jnp.logical_and(active, x == z0))
+    away_at = [jnp.logical_and(away, c == i) for i in range(2)]
+    core_is = [c == 0, c == 1]
+    holds = [jnp.logical_and(holder, c == i) for i in range(2)]
+    small_cols = [block(row, slim) for row in row_peers]
+
+    sems = {}
+    pending = {}
+
+    def remote(name, src, dst, device):
+        at = sems.setdefault(name, len(sems))
+        assert at < N_SEM
+        return pltpu.make_async_remote_copy(
+            src_ref=taken(src),
+            dst_ref=taken(dst),
+            send_sem=k.send.at[at],
+            recv_sem=k.recv.at[at],
+            device_id=device,
+            device_id_type=MESH,
+        )
+
+    def when(cond, go):
+        if cond is None:
+            go()
+        else:
+            pl.when(cond)(go)
+
+    def post(name, src, dst, device, cond=None):
+        when(cond, lambda: remote(name, src, dst, device).start())
+        pending[name] = cond, (name, src, dst, device)
+
+    def left(name):
+        cond, args = pending.pop(name)
+        when(cond, lambda: remote(*args).wait_send())
+
+    def arrived(name, dst):
+        remote(name, dst, dst, to_c).wait_recv()
+
+    local_count = [0]
+
+    def local_copy(src, dst):
+        at = local_count[0]
+        local_count[0] += 1
+        return pltpu.make_async_copy(taken(src), taken(dst), k.local.at[at])
+
+    def fetch(src, dst):
+        copy = local_copy(src, dst)
+        copy.start()
+        return copy
+
+    stored = []
+
+    def put(src, dst, cond=None):
+        at = local_count[0]
+        local_count[0] += 1
+
+        def copy():
+            return pltpu.make_async_copy(taken(src), taken(dst), k.local.at[at])
+
+        when(cond, lambda: copy().start())
+        stored.append((cond, copy))
+
+    def add(dst, src):
+        dst[...] = (dst[...].astype(F32) + src[...].astype(F32)).astype(BF)
+
+    def chosen(rel, bit):
+        return bit if rel else 1 - bit
+
+    class Travel:
+        def __init__(self, tag, own):
+            self.tag, self.own, self.order = tag, own, STAGES[tag]
+            self.counts = counts_of(tag)
+            self.got = travelling[N.got, tag]
+            self.starts = [sum(self.counts[1 : p + 1]) for p in range(len(self.order))]
+            self.alive = active if tag in DOWN else holder
+            self.role_at = len(self.order)
+            for p, dim in enumerate(self.order):
+                if dim not in scatter_of(tag):
+                    self.role_at = p
+
+        def held(self, p, i):
+            return (self.own, i) if p == 0 else (self.got, self.starts[p - 1] + i)
+
+        def leave(self, p, i):
+            if p == len(self.order):
+                return
+            dim = self.order[p]
+            ref, at = self.held(p, i)
+            cond = None
+            if dim in scatter_of(self.tag):
+                if i >= self.counts[p] // 2:
+                    return
+                if p > self.role_at:
+                    cond = self.alive
+            else:
+                cond = idle if self.tag in DOWN else lender
+            post((self.tag, p, i), At(ref)[at], At(self.got)[self.starts[p] + i], to_dim[dim], cond)
+
+        def step(self, p, i):
+            at = self.starts[p] + i
+            halved = self.order[p] in scatter_of(self.tag)
+            ref, mine = self.held(p, i + (self.counts[p + 1] if halved else 0))
+
+            def go():
+                arrived((self.tag, p, i), At(self.got)[at])
+                add(self.got.at[at], ref.at[mine])
+
+            when(self.alive if p >= self.role_at else None, go)
+            self.leave(p + 1, i)
+
+        def last(self):
+            return At(self.got)[self.starts[-1]]
+
+    travels = {tag: Travel(tag, travelling.get((N.own, tag))) for tag in STAGES}
+    steps = {}
+    for tag, travel in travels.items():
+        for p in range(len(travel.order)):
+            for i in range(travel.counts[p + 1]):
+                steps[tag, p, i] = functools.partial(travel.step, p, i)
+
+    got_tok = fetch(k.tokens.at[0], k.tok)
+    got_cot = fetch(k.cotangent.at[0], k.cot)
+    barrier = pltpu.get_barrier_semaphore()
+    for device in partners:
+        pl.semaphore_signal(barrier, inc=1, device_id=device, device_id_type=MESH)
+
+    position = s * span + lax.broadcasted_iota(jnp.int32, (span, 1), 0)
+    starts = [np.int32(0)]
+    for i in range(k.lengths.shape[1] - 1):
+        starts.append(starts[-1] + k.lengths[0, i])
+
+    def first_of(at):
+        first = jnp.zeros_like(at)
+        for start in starts:
+            first = jnp.maximum(first, jnp.where(start <= at, start, 0))
+        return first
+
+    def flag(test):
+        return jnp.where(test, 1.0, 0.0).astype(F32)
+
+    def write_masks():
+        first0, first1, first2 = (first_of(position + i) for i in range(3))
+        columns = [
+            flag(position < k.counts[0]),
+            flag(position >= first0),
+            flag(position - 1 >= first0),
+            flag(position - 2 >= first0),
+            flag(position >= first1),
+            flag(position >= first2),
+        ]
+        lane = lax.broadcasted_iota(jnp.int32, (span, 128), 1)
+        table = jnp.zeros((span, 128), F32)
+        for i, column in enumerate(columns):
+            table = jnp.where(lane == i, column, table)
+        k.mask[...] = table
+
+    def mask(i, rows=slice(None)):
+        return k.mask[rows, i : i + 1]
+
+    def gain(ref):
+        return ref[...].astype(F32)
+
+    step = 64
+    passes = span // step
+    part = span // 2
+
+    def mixer_forward(win):
+        got_win = [fetch(k.w_in.at[:, block(i, width)], win.at[:, block(i, width)]) for i in (0, 2, 1)]
+        got_wout = fetch(k.w_out, k.wout)
+        write_masks()
+        got_tok.wait()
+
+        @functools.partial(loop, passes, unroll=False)
+        def _(i):
+            rows = block(i, step)
+            t = k.tok[rows, :].astype(F32)
+            scale = lax.rsqrt(jnp.mean(t * t, axis=-1, keepdims=True) + EPSILON)
+            k.sc1[rows, :] = scale
+            k.nrm[rows, :] = (t * scale * gain(k.gain1)).astype(BF)
+
+        got_cot.wait()
+
+        @functools.partial(loop, passes, unroll=False)
+        def _(i):
+            rows = block(i, step)
+            k.df[rows, :] = (mask(MASK_VALID, rows) * k.cot[rows, :].astype(F32)).astype(BF)
+
+        pl.semaphore_wait(barrier, len(partners))
+        post(
+            N.df_z(0),
+            At(k.df)[pl.ds(0, span), first_cols],
+            At(k.df)[pl.ds(2 * span, span), first_cols],
+            to_z,
+        )
+        post(N.df_c, At(k.df)[pl.ds(0, span)], At(k.df)[pl.ds(span, span)], to_c)
+        got_win[0].wait()
+        got_win[1].wait()
+
+        @functools.partial(loop, width // 256)
+        def _(j):
+            n = k.nrm[:span, :]
+            cols = block(j, 256)
+            gb = dot(n, win[:, cols])
+            va = dot(n, win[:, pl.ds(pl.multiple_of(2 * width + j * 256, 256), 256)])
+            k.gb[:, cols] = gb.astype(BF)
+            k.va[:, cols] = va.astype(BF)
+            k.mix[8:, cols] = (mask(MASK_VALID) * gb * va).astype(BF).astype(F32)
+
+        post(N.halo, At(k.mix)[pl.ds(span, 8)], k.hr, after, not_last)
+        got_win[2].wait()
+
+        @functools.partial(loop, width // 256)
+        def _(j):
+            cols = block(j, 256)
+            c_cols = pl.ds(pl.multiple_of(width + j * 256, 256), 256)
+            k.gc[:, cols] = dot(k.nrm[:span, :], win[:, c_cols])
+
+        got_wout.wait()
+
+    pl.run_scoped(mixer_forward, pltpu.VMEM((width, 3 * width), BF))
+
+    @pl.when(s == 0)
+    def _():
+        k.mix[:8, :] = jnp.zeros((8, width), F32)
+
+    @pl.when(not_first)
+    def _():
+        arrived(N.halo, k.hr)
+        k.mix[:8, :] = k.hr[...]
+
+    def tap(i, cols):
+        return k.taps[i : i + 1, cols].astype(F32)
+
+    def conv_of(cols):
+        return (
+            tap(0, cols) * mask(MASK_S0) * k.mix[8 : 8 + span, cols]
+            + tap(1, cols) * mask(MASK_S1) * k.mix[7 : 7 + span, cols]
+            + tap(2, cols) * mask(MASK_S2) * k.mix[6 : 6 + span, cols]
+        )
+
+    @functools.partial(loop, width // 256, unroll=False)
+    def _(j):
+        cols = block(j, 256)
+        k.gat[:span, cols] = (mask(MASK_VALID) * k.gc[:, cols] * conv_of(cols)).astype(BF)
+
+    @functools.partial(loop, width // 256)
+    def _(j):
+        cols = block(j, 256)
+        k.res[:, cols] = k.tok[:, cols].astype(F32) + dot(k.gat[:span, :], k.wout[:, cols])
+
+    for i in range(2):
+
+        @functools.partial(loop, passes // 2, unroll=False)
+        def _(j):
+            rows = block(i * (passes // 2) + j, step)
+            v = k.res[rows, :]
+            scale = lax.rsqrt(jnp.mean(v * v, axis=-1, keepdims=True) + EPSILON)
+            k.sc2[rows, :] = scale
+            k.n2[rows, :] = (v * scale * gain(k.gain2)).astype(BF)
+
+        here = pl.ds(i * part, part)
+        post(N.n2_z(i), At(k.n2)[here], At(k.n2)[pl.ds(2 * span + i * part, part)], to_z)
+    post(N.n2_c, At(k.n2)[pl.ds(0, span)], At(k.n2)[pl.ds(span, span)], to_c)
+    post(
+        N.df_z(1),
+        At(k.df)[pl.ds(0, span), last_cols],
+        At(k.df)[pl.ds(2 * span, span), last_cols],
+        to_z,
+    )
+    post(N.nrm_c, At(k.nrm)[pl.ds(0, span)], At(k.nrm)[pl.ds(span, span)], to_c)
+    post(N.gat_c, At(k.gat)[pl.ds(0, span)], At(k.gat)[pl.ds(span, span)], to_c)
+
+    z_rows, t_rows = pl.ds(2 * span, span), pl.ds(3 * span, span)
+    z_parts = [pl.ds(2 * span + i * part, part) for i in range(2)]
+    t_parts = [pl.ds(3 * span + i * part, part) for i in range(2)]
+    half_cols = (first_cols, last_cols)
+
+    def pass_df(i):
+        arrived(N.df_z(i), At(k.df)[z_rows, half_cols[i]])
+        post(N.df_t(i), At(k.df)[z_rows, half_cols[i]], At(k.df)[t_rows, half_cols[i]], to_c)
+
+    def pass_n2(i):
+        arrived(N.n2_z(i), At(k.n2)[z_parts[i]])
+        post(N.n2_t(i), At(k.n2)[z_parts[i]], At(k.n2)[t_parts[i]], to_c)
+
+    for i in range(2):
+        steps[N.tdf(i)] = functools.partial(pass_df, i)
+        steps[N.tn(i)] = functools.partial(pass_n2, i)
+
+    def down_last(i):
+        got = travels[DOWN[i]].last()
+        post(N.rd4(i), got, k.rd4, targets[i], gives[i])
+        put(got, k.g_down, home[i])
+
+    def down_take():
+        for i in range(2):
+            when(away_at[i], lambda: arrived(N.rd4(i), k.rd4))
+        put(k.rd4, k.g_down, away)
+
+    def wide_last(tag):
+        mine, out = (k.rg4, k.g_gate) if tag == N.g else (k.ru4, k.g_up)
+        for core in range(2):
+            got = travels[(GATE if tag == N.g else UP)[core]].last()
+            post((tag, core), got, mine, to_c, holds[1 - core])
+            put(got, out, holds[core])
+
+    lends = [jnp.logical_and(lender, c == i) for i in range(2)]
+
+    def wide_take(tag):
+        mine, out = (k.rg4, k.g_gate) if tag == N.g else (k.ru4, k.g_up)
+        for core in range(2):
+            when(lends[core], lambda: arrived((tag, core), mine))
+        put(mine, out, lender)
+
+    for i in range(2):
+        steps[N.dl(i)] = functools.partial(down_last, i)
+    steps[N.dt] = down_take
+    for tag in (N.g, N.u):
+        steps[N.w3(tag)] = functools.partial(wide_last, tag)
+        steps[N.w4(tag)] = functools.partial(wide_take, tag)
+
+    def small_rows():
+        total = k.sg[:, small_cols[0]]
+        for i in range(1, 8):
+            arrived(N.sa(i), At(k.sa)[i - 1])
+            total = total + k.sa[i - 1]
+        k.ss[...] = total
+        for i in range(1, 4):
+            post(N.sb(i), k.ss, At(k.sb)[i - 1], (r, seq_peers[i]))
+
+    def small_seq():
+        total = k.ss[...]
+        for i in range(1, 4):
+            arrived(N.sb(i), At(k.sb)[i - 1])
+            left(N.sb(i))
+            total = total + k.sb[i - 1]
+        k.ss[...] = total
+        put(k.ss, k.small)
+
+    steps[N.sg(0)], steps[N.sg(1)] = small_rows, small_seq
+
+    def layer_output():
+        arrived(N.fz, k.fz)
+
+        @functools.partial(loop, passes, unroll=False)
+        def _(i):
+            rows = block(i, step)
+            valid = mask(MASK_VALID, rows)
+            k.cot[rows, :] = (k.loa[rows, :] + valid * k.fz[rows, :].astype(F32)).astype(BF)
+
+        put(k.cot, k.layer_out.at[0])
+
+    steps[N.lo] = layer_output
+    feed_end = 1 + max(i for i, name in enumerate(ORDER) if name[0] in FEED)
+
+    def feed_forward(wg, wu, wd, hid, dg, du):
+        q = 2 * c + z0
+        got_wg = fetch(k.w_gate.at[:, block(q, quarter)], wg)
+        got_wu = fetch(k.w_up.at[:, block(q, quarter)], wu)
+        got_wd = fetch(k.w_down.at[block(q, quarter), :], wd)
+
+        def tiles(body, unroll):
+            loop(quarter // 256, lambda j: body(block(j, 256)), unroll)
+            if quarter % 256:
+                body(pl.ds(quarter - quarter % 256, quarter % 256))
+
+        def expand(rows, unroll):
+            def tile(cols):
+                n = k.n2[rows, :]
+                g = dot(n, wg[:, cols])
+                u = dot(n, wu[:, cols])
+                sig = jax.nn.sigmoid(g)
+                silu = g * sig
+                hid[rows, cols] = (silu * u).astype(BF)
+                dg[rows, cols] = (u * sig * (1.0 + g * (1.0 - sig))).astype(BF)
+                du[rows, cols] = silu.astype(BF)
+
+            tiles(tile, unroll)
+
+        def retreat(slot, unroll):
+            rows = pl.ds(slot * span, span)
+
+            def tile(cols):
+                d = dot_nt(k.df[rows, :], wd[cols, :])
+                dg[rows, cols] = (d * dg[rows, cols].astype(F32)).astype(BF)
+                du[rows, cols] = (d * du[rows, cols].astype(F32)).astype(BF)
+
+            tiles(tile, unroll)
+
+        def back(slot, ref, plus, unroll):
+            rows = pl.ds(slot * span, span)
+
+            @functools.partial(loop, width // 256, unroll=unroll)
+            def _(j):
+                cols = block(j, 256)
+                value = dot_nt(dg[rows, :], wg[cols, :]) + dot_nt(du[rows, :], wu[cols, :])
+                if plus is not None:
+                    value = value + plus[:, cols].astype(F32)
+                ref[:, cols] = value.astype(ref.dtype)
+
+        def forth(slot, store):
+            rows = pl.ds(slot * span, span)
+
+            @functools.partial(loop, width // 256, unroll=False)
+            def _(j):
+                cols = block(j, 256)
+                store(cols, dot(hid[rows, :], wd[:, cols]))
+
+        own = steps
+
+        def ex0():
+            got_wg.wait()
+            got_wu.wait()
+            expand(pl.ds(0, span), False)
+
+        def ex1():
+            arrived(N.n2_c, At(k.n2)[pl.ds(span, span)])
+            expand(pl.ds(span, span), False)
+
+        def re0():
+            got_wd.wait()
+            retreat(0, False)
+
+        def re1():
+            arrived(N.df_c, At(k.df)[pl.ds(span, span)])
+            retreat(1, False)
+
+        def bk1():
+            back(1, k.ps.at[0], None, False)
+            post(N.pr0, At(k.ps)[0], At(k.pr)[0], to_c)
+
+        def bk0():
+            arrived(N.pr0, At(k.pr)[0])
+            back(0, k.own, k.pr.at[0], False)
+
+        def ex2(i):
+            expand(z_parts[i], True)
+
+        def ex3(i):
+            arrived(N.n2_t(i), At(k.n2)[t_parts[i]])
+            expand(t_parts[i], True)
+
+        def bk3():
+            back(3, k.ps.at[1], None, True)
+            post(N.pr1, At(k.ps)[1], At(k.pr)[1], to_c)
+
+        def bk2():
+            arrived(N.pr1, At(k.pr)[1])
+            back(2, k.pr.at[1], k.pr.at[1], True)
+            post(N.pz, At(k.pr)[1], k.pz, to_z)
+
+        def wide_grad(tag, core, u, grad):
+            travel = travels[tag]
+            rel = unit_bits(tag, u)
+            rho = 4 * chosen(rel[N.y], y) + 2 * chosen(rel[N.x], x) + core
+            travel.own[u] = dot_tn(k.n2[:, block(rho, slim)], grad[...]).astype(BF)
+            travel.leave(0, u)
+
+        def to_ref(ref, plus=None):
+            def store(cols, value):
+                if plus is not None:
+                    value = value + plus[:, cols].astype(F32)
+                ref[:, cols] = value.astype(ref.dtype)
+
+            return store
+
+        def fo1():
+            left(N.pr0)
+            forth(1, to_ref(k.ps.at[0]))
+            post(N.fr0, At(k.ps)[0], At(k.fr)[0], to_c)
+
+        def fo3():
+            left(N.pr1)
+            forth(3, to_ref(k.ps.at[1]))
+            post(N.fr1, At(k.ps)[1], At(k.fr)[1], to_c)
+
+        def fo2():
+            arrived(N.fr1, At(k.fr)[1])
+            forth(2, to_ref(k.fr.at[1], k.fr.at[1]))
+            post(N.fz, At(k.fr)[1], k.fz, to_z)
+
+        def fo0():
+            arrived(N.fr0, At(k.fr)[0])
+
+            def store(cols, value):
+                value = value + k.fr[0, :, cols].astype(F32)
+                k.loa[:, cols] = k.res[:, cols] + mask(MASK_VALID) * value
+
+            forth(0, store)
+
+        own.update({N.ex(0): ex0, N.ex(1): ex1, N.re(0): re0, N.re(1): re1})
+        own.update({N.bk(0): bk0, N.bk(1): bk1, N.bk(2): bk2, N.bk(3): bk3})
+        own.update({N.fo(0): fo0, N.fo(1): fo1, N.fo(2): fo2, N.fo(3): fo3})
+        own[N.re(2)] = functools.partial(retreat, 2, True)
+
+        def re3():
+            arrived_df1()
+            retreat(3, True)
+
+        seen = []
+
+        def arrived_df1():
+            if not seen:
+                seen.append(1)
+                arrived(N.df_t(1), At(k.df)[t_rows, half_cols[1]])
+
+        def dn1():
+            arrived_df1()
+            grads_down(1)
+
+        def dn0():
+            arrived(N.df_t(0), At(k.df)[t_rows, half_cols[0]])
+            grads_down(0)
+
+        def grads_down(rel_w):
+            for rel_x in range(2):
+                sigma = 2 * chosen(rel_w, z1) + chosen(rel_x, x)
+                value = dot_tn(hid[...], k.df[:, block(sigma, side)])
+                for i, tag in enumerate(DOWN):
+                    u = unit_index(tag, {N.x: rel_x, N.z1: rel_w})
+                    travels[tag].own[u] = value[i * tall : (i + 1) * tall].astype(BF)
+                    travels[tag].leave(0, u)
+
+        own.update({N.re(3): re3, N.dn(0): dn0, N.dn(1): dn1})
+        for i in range(2):
+            own[N.ex(2, i)] = functools.partial(ex2, i)
+            own[N.ex(3, i)] = functools.partial(ex3, i)
+            for u in range(4):
+                own[N.gg(i, u)] = functools.partial(wide_grad, GATE[i], i, u, dg)
+                own[N.uu(i, u)] = functools.partial(wide_grad, UP[i], i, u, du)
+        for name in ORDER[:feed_end]:
+            own[name]()
+
+    pl.run_scoped(
+        feed_forward,
+        pltpu.VMEM((width, quarter), BF),
+        pltpu.VMEM((width, quarter), BF),
+        pltpu.VMEM((quarter, width), BF),
+        pltpu.VMEM((4 * span, quarter), BF),
+        pltpu.VMEM((4 * span, quarter), BF),
+        pltpu.VMEM((4 * span, quarter), BF),
+    )
+
+    def mixer_backward(win, gm):
+        got_win = fetch(k.w_in, win)
+        share = slim // len(MIXED)
+        for h, tag in enumerate(MIXED):
+            travels[tag].own = gm.at[h]
+
+        def mb1():
+            arrived(N.pz, k.pz)
+            k.sg[...] = jnp.zeros((8, width), F32)
+
+            @functools.partial(loop, passes, unroll=False)
+            def _(i):
+                rows = block(i, step)
+                d = k.own[rows, :] + k.pz[rows, :].astype(F32)
+                v = k.res[rows, :]
+                scale = k.sc2[rows, :]
+                scaled = gain(k.gain2) * d
+                k.sg[1:2, :] = k.sg[1:2, :] + jnp.sum(d * v * scale, axis=0, keepdims=True)
+                d = (
+                    k.cot[rows, :].astype(F32)
+                    + scale * scaled
+                    - v * (scale * scale * scale) * jnp.mean(scaled * v, axis=-1, keepdims=True)
+                )
+                k.own[rows, :] = d
+                k.dmx[rows, :] = d.astype(BF)
+
+            post(N.dmx_c, At(k.dmx)[pl.ds(0, span)], At(k.dmx)[pl.ds(span, span)], to_c)
+
+        def mb2():
+            @functools.partial(loop, width // 256)
+            def _(j):
+                cols = block(j, 256)
+                d = dot_nt(k.dmx[:span, :], k.wout[cols, :])
+                valid = mask(MASK_VALID)
+                k.dc[:span, cols] = (valid * k.gc[:, cols] * d).astype(BF).astype(F32)
+                c_cols = pl.ds(pl.multiple_of(width + j * 256, 256), 256)
+                k.dpj[:span, c_cols] = (valid * conv_of(cols) * d).astype(BF)
+
+            post(N.halo2, At(k.dc)[pl.ds(0, 8)], k.hr2, before, not_first)
+
+        def mb3():
+            @pl.when(s == 3)
+            def _():
+                k.dc[span:, :] = jnp.zeros((8, width), F32)
+
+            @pl.when(not_last)
+            def _():
+                arrived(N.halo2, k.hr2)
+                k.dc[span:, :] = k.hr2[...]
+
+            @functools.partial(loop, width // 256, unroll=False)
+            def _(j):
+                cols = block(j, 256)
+                d0 = k.dc[:span, cols]
+                d = (
+                    tap(0, cols) * mask(MASK_S0) * d0
+                    + tap(1, cols) * mask(MASK_N1) * k.dc[1 : 1 + span, cols]
+                    + tap(2, cols) * mask(MASK_N2) * k.dc[2 : 2 + span, cols]
+                )
+                valid = mask(MASK_VALID)
+                k.dpj[:span, cols] = (valid * k.va[:, cols].astype(F32) * d).astype(BF)
+                x_cols = pl.ds(pl.multiple_of(2 * width + j * 256, 256), 256)
+                k.dpj[:span, x_cols] = (valid * k.gb[:, cols].astype(F32) * d).astype(BF)
+                for i, m in ((0, MASK_S0), (1, MASK_S1), (2, MASK_S2)):
+                    k.sg[2 + i : 3 + i, cols] = jnp.sum(
+                        d0 * mask(m) * k.mix[8 - i : 8 - i + span, cols], axis=0, keepdims=True
+                    )
+
+            post(N.dpj_c, At(k.dpj)[pl.ds(0, span)], At(k.dpj)[pl.ds(span, span)], to_c)
+
+        def mb4():
+            got_win.wait()
+
+            @functools.partial(loop, width // 256)
+            def _(j):
+                cols = block(j, 256)
+                k.gc[:, cols] = dot_nt(k.dpj[:span, :], win[cols, :])
+
+            @functools.partial(loop, passes, unroll=False)
+            def _(i):
+                rows = block(i, step)
+                d = k.gc[rows, :]
+                t = k.tok[rows, :].astype(F32)
+                scale = k.sc1[rows, :]
+                scaled = gain(k.gain1) * d
+                k.sg[0:1, :] = k.sg[0:1, :] + jnp.sum(d * t * scale, axis=0, keepdims=True)
+                d = (
+                    k.own[rows, :]
+                    + scale * scaled
+                    - t * (scale * scale * scale) * jnp.mean(scaled * t, axis=-1, keepdims=True)
+                )
+                k.tok[rows, :] = d.astype(BF)
+
+            put(k.tok, k.grad_tokens.at[0])
+            for i in range(1, 8):
+                post(N.sa(i), At(k.sg)[:, small_cols[i]], At(k.sa)[i - 1], (row_peers[i], s))
+            for name, ref in (
+                (N.nrm_c, k.nrm),
+                (N.gat_c, k.gat),
+                (N.dmx_c, k.dmx),
+                (N.dpj_c, k.dpj),
+            ):
+                arrived(name, At(ref)[pl.ds(span, span)])
+
+        def mg(rel_x, rel_y):
+            rho = 4 * chosen(rel_y, y) + 2 * chosen(rel_x, x) + c
+            rows = block(rho, slim)
+            leaving = []
+            for a in range(2):
+                for b in range(2):
+                    sigma = 2 * chosen(b, z1) + chosen(a, z0)
+                    first = dot_tn(k.nrm[:, rows], k.dpj[:, block(sigma, wide)])
+                    second = dot_tn(k.gat[:, rows], k.dmx[:, block(sigma, side)])
+                    for h, tag in enumerate(MIXED):
+                        u = unit_index(tag, {N.x: rel_x, N.y: rel_y, N.z0: a, N.z1: b})
+                        here = slice(h * share, (h + 1) * share)
+                        gm[h, u, :, :wide] = first[here].astype(BF)
+                        gm[h, u, :, wide:] = second[here].astype(BF)
+                        leaving.append((u, tag, h))
+            for u, tag, h in sorted(leaving):
+                leave_mixed(tag, h, u)
+
+        def leave_mixed(tag, h, u):
+            travel = travels[tag]
+            if u < travel.counts[0] // 2:
+                dst = At(travel.got)[travel.starts[0] + u]
+                post((tag, 0, u), At(gm)[h, u], dst, to_dim[travel.order[0]])
+
+        def finish_mixed():
+            for h, tag in enumerate(MIXED):
+                got, at = travels[tag].got, travels[tag].starts[-1]
+                rows = pl.ds(h * share, share)
+                put(At(got)[at, :, pl.ds(0, wide)], At(k.g_in)[rows, :])
+                put(At(got)[at, :, pl.ds(wide, width - wide)], At(k.g_out)[rows, :])
+
+        steps.update({N.mb(1): mb1, N.mb(2): mb2, N.mb(3): mb3, N.mb(4): mb4})
+        for a in range(2):
+            for b in range(2):
+                steps[N.mg(a, b)] = functools.partial(mg, a, b)
+        for name in ORDER[feed_end:]:
+            steps[name]()
+        finish_mixed()
+        for name in list(pending):
+            left(name)
+        for cond, copy in stored:
+            when(cond, lambda: copy().wait())
+
+    pl.run_scoped(
+        mixer_backward,
+        pltpu.VMEM((width, 3 * width), BF),
+        pltpu.VMEM((len(MIXED), 16, slim // len(MIXED), width), BF),
+    )
+
+
+def finish_kernel(n, *refs):
+    sources, small = refs[:n], refs[n]
+    targets, smalls = refs[n + 1 : 2 * n + 1], refs[2 * n + 1 : 2 * n + 4]
+    rest = refs[2 * n + 4 :]
+    held, wide, gets, puts = rest[:n], rest[n : 2 * n], rest[2 * n], rest[2 * n + 1]
+    copies = [pltpu.make_async_copy(sources[i], held[i], gets.at[i]) for i in range(n)]
+    for copy in copies:
+        copy.start()
+    s = lax.axis_index("seq")
+    piece = smalls[0].shape[-1]
+    value = jnp.zeros((8, piece), F32)
+    for i in range(small.shape[1] // piece):
+        value = jnp.where(s == i, small[:, i * piece : (i + 1) * piece], value)
+    smalls[0][...] = value[0:1]
+    smalls[1][...] = value[2:5]
+    smalls[2][...] = value[1:2]
+    out = []
+    for i in range(n):
+        copies[i].wait()
+        ref = held[i]
+        if sources[i].dtype != targets[i].dtype:
+            rows = 64
+
+            @functools.partial(loop, ref.shape[0] // rows, unroll=False)
+            def _(j):
+                here = block(j, rows)
+                wide[i][here, :] = ref[here, :].astype(F32)
+
+            ref = wide[i]
+        copy = pltpu.make_async_copy(ref, targets[i], puts.at[i])
+        copy.start()
+        out.append(copy)
+    for copy in out:
+        copy.wait()
+
+
+def fused(
+    tokens,
+    doc_lengths,
+    valid_counts,
+    norm_in,
+    w_in,
+    w_conv,
+    w_out,
+    norm_ffn,
+    w_gate,
+    w_up,
+    w_down,
+    cotangent,
+):
+    _, span, width = tokens.shape
+    ff = w_gate.shape[1]
+    rows, seq = lax.axis_size("rows"), lax.axis_size("seq")
+    scratch = scratch_list(span, width, ff, rows, seq)
+    anywhere = pl.BlockSpec(memory_space=pl.ANY)
+    scalars = pl.BlockSpec(memory_space=pltpu.SMEM)
+    vectors = pl.BlockSpec(memory_space=pltpu.VMEM)
+    grads = [
+        (width // rows, 3 * width // seq),
+        (width // rows, width // seq),
+        (width // rows, ff // seq),
+        (width // rows, ff // seq),
+        (ff // rows, width // seq),
+    ]
+    *outs, small = pl.pallas_call(
+        functools.partial(layer_kernel, OPERANDS + list(scratch)),
+        out_shape=[jax.ShapeDtypeStruct((1, span, width), BF)] * 2
+        + [jax.ShapeDtypeStruct(shape, BF) for shape in grads]
+        + [jax.ShapeDtypeStruct((8, width // rows), F32)],
+        in_specs=[scalars] * 2 + [anywhere] * 2 + [vectors] * 3 + [anywhere] * 5,
+        out_specs=[anywhere] * 8,
+        scratch_shapes=list(scratch.values()),
+        compiler_params=pltpu.CompilerParams(
+            collective_id=0, has_side_effects=True, vmem_limit_bytes=67043328
+        ),
+        name="layer",
+    )(
+        doc_lengths,
+        valid_counts,
+        tokens,
+        cotangent,
+        norm_in[None],
+        w_conv,
+        norm_ffn[None],
+        w_in,
+        w_out,
+        w_gate,
+        w_up,
+        w_down,
+    )
+    piece = width // (rows * seq)
+    n = len(outs)
+    held = [(1, span, width)] * 2 + grads
+    *final, first, taps, second = pl.pallas_call(
+        functools.partial(finish_kernel, n),
+        out_shape=[jax.ShapeDtypeStruct((1, span, width), BF)] * 2
+        + [jax.ShapeDtypeStruct(shape, F32) for shape in grads]
+        + [jax.ShapeDtypeStruct((i, piece), F32) for i in (1, 3, 1)],
+        in_specs=[anywhere] * n + [vectors],
+        out_specs=[anywhere] * n + [vectors] * 3,
+        scratch_shapes=[pltpu.VMEM(shape, BF) for shape in held]
+        + [pltpu.VMEM(shape if i > 1 else (8, 128), F32) for i, shape in enumerate(held)]
+        + [pltpu.SemaphoreType.DMA((n,))] * 2,
+        name="finish",
+    )(*outs, small)
+    layer_out, grad_tokens, g_in, g_out, g_gate, g_up, g_down = final
+    return (
+        layer_out,
+        grad_tokens,
+        first[0],
+        g_in,
+        taps,
+        g_out,
+        second[0],
+        g_gate,
+        g_up,
+        g_down,
     )
 
 
@@ -212,8 +1238,9 @@
         P(),
         P("rows", "seq", None),
     )
+    paired = mesh.shape["rows"] == 8 and mesh.shape["seq"] == 4
     return jax.shard_map(
-        local,
+        fused if paired else plain,
         mesh=mesh,
         in_specs=placed,
         out_specs=(

time: 627 us -> 152 us (0.24)
  waiting for transfers between devices: 456 us -> 0 us
  Pallas kernels: 0 us -> 147 us
  matrix products: 85.6 us -> 0 us
  blocking collectives: 24.4 us -> 0 us
  other arithmetic: 21.2 us -> 0 us
  between operations: 16.7 us -> 1.5 us
  local copies, waits for them, and re-layouts: 15.5 us -> 2.56 us
  starting transfers between devices: 7.1 us -> 0 us
    reduce_scatter x8 -> x0, waiting for transfers between devices: 392 us -> none  [the longest x1 80.2 us: local(): lax.psum_scatter(grad_w_gate.astype(jnp.bfloat16), 'rows', scatter_dimens...]
    pallas_call x0 -> x2, Pallas kernels: none -> 147 us  [the longest x1 143 us: fused(): pl.pallas_call(functools.partial(layer_kernel, OPERANDS + list(scratch)),...]
    dot_general x15 -> x0, matrix products: 85.6 us -> none  [the longest x5 30.7 us: back_product(): jnp.einsum('tb,ab->ta', grad, weight, preferred_element_type=jnp.float32)]
    unnamed x16 -> x0, waiting for transfers between devices: 59.2 us -> none
    unnamed x2 -> x0, blocking collectives: 24.4 us -> none
    unnamed x74 -> x0, local copies, waits for them, and re-layouts: 15.4 us -> none
    convert_element_type x16 -> x0, other arithmetic: 11.9 us -> none  [the longest x8 8.48 us: local(): sum_gain_in, sum_in, sum_conv, sum_out, sum_gate, sum_up, sum_down, sum_g...]
    ppermute x2 -> x0, starting transfers between devices: 6.39 us -> none  [passed_along(): lax.ppermute(value, axis, [(source, source + steps) for source in range(f...]
  transfers between devices with their start and end apart: 14 -> 0, of which waited for: 12 -> 0; matrix products, arithmetic and copies ran while one was open for 10% -> 0% of each run, Pallas kernels for 0% -> 0%
where the time goes in v2:
time: 152 us; the launch traced here: 151 us
  Pallas kernels  147 us (97%)
  local copies, waits for them, and re-layouts  2.56 us (2%)
    pallas_call x1, Pallas kernels, fused(): pl.pallas_call(functools.partial(layer_kernel, OPERANDS + list(scratch)),...  143 us
    pallas_call x1, Pallas kernels, fused(): pl.pallas_call(functools.partial(finish_kernel, n), out_shape=[jax.ShapeD...  4.15 us

profile of v2, /device:TPU:0, one launch (start us, length us, event | category | flops | bytes accessed | tf_op | source)
XLA Modules:
  0.0 151.3 jit_solution(11275202810901967334)
XLA Ops:
  1.3 1.3 broadcast_in_dim.6.refs_4_
  2.6 1.3 broadcast_in_dim.7.refs_6_
  3.8 143.1 %layer.1 = (bf16[1,256,1024]{2,1,0:T(8,128)(2,1)}, bf16[1,256,1024]{2,1,0:T(8,128)(2,1)}, bf16[128,768]{1,0:T(8,128)(2,1)}, bf16[128,256]{1,0:T(8,128)(2,1)}, bf...) custom-call(s32[1,8]{1,0:T(1,128)} %refs_0_.1, ...), custom_call_target="tpu_custom_call" | custom-call | tf_op jit(solution)/shard_map/layer/pallas_call | solution.py:1170
  146.9 4.1 %finish.1 = (bf16[1,256,1024]{2,1,0:T(8,128)(2,1)}, bf16[1,256,1024]{2,1,0:T(8,128)(2,1)}, f32[128,768]{1,0:T(8,128)}, f32[128,256]{1,0:T(8,128)}, f32[128,1152]...) custom-call(bf16[1,256,1024]{2,1,0:T(8,128)(2,1)} %get-tuple-element, ...), custom_call_target="tpu_custom_call" | custom-call | tf_op jit(solution)/shard_map/finish/pallas_call | solution.py:1199

commit v3 on v2

--- a/solution.py
+++ b/solution.py
@@ -206,31 +206,45 @@
     N.A: (N.x, N.y, N.z1),
     N.B: (N.y, N.z1, N.x),
     N.g0: (N.y, N.x, N.z1),
-    N.g1: (N.x, N.y, N.z1),
-    N.u0: (N.x, N.y, N.z1),
+    N.g1: (N.y, N.x, N.z1),
+    N.u0: (N.x, N.z1, N.y),
     N.u1: (N.x, N.y, N.z1),
     N.m0: (N.y, N.x, N.z0, N.z1),
-    N.m1: (N.y, N.x, N.z0, N.z1),
+    N.m1: (N.x, N.z0, N.y, N.z1),
+    N.m2: (N.z0, N.x, N.z1, N.y),
 }
 ORDER = [
-    N.ex(0), N.tdf(0), N.re(0), N.ex(1), N.re(1), N.bk(1), N.bk(0), N.tn(0),
-    N.ex(2, 0), N.ex(3, 0), N.tn(1), N.ex(2, 1), N.ex(3, 1), N.dn(0), N.tdf(1), N.re(2),
-    N.re(3), N.dn(1), N.B(0, 0), N.bk(3), N.gg(0, 0), N.uu(0, 0), N.gg(1, 0), N.A(0, 0),
-    N.B(0, 1), N.uu(1, 0), N.bk(2), N.gg(0, 1), N.uu(0, 1), N.gg(1, 1), N.uu(1, 1), N.gg(0, 2),
-    N.uu(0, 2), N.gg(1, 2), N.uu(1, 2), N.gg(0, 3), N.uu(0, 3), N.B(0, 2), N.gg(1, 3), N.uu(1, 3),
-    N.A(0, 1), N.fo(1), N.B(1, 0), N.fo(3), N.fo(2), N.fo(0), N.B(0, 3), N.g0(0, 0),
-    N.u0(0, 0), N.B(1, 1), N.g1(0, 0), N.mb(1), N.mb(2), N.g0(0, 1), N.A(1, 0), N.u1(0, 0),
-    N.mb(3), N.mb(4), N.lo, N.u0(0, 1), N.mg(0, 0), N.mg(0, 1), N.u0(1, 0), N.mg(1, 0),
-    N.A(1, 1), N.mg(1, 1), N.g1(0, 1), N.A(2, 0), N.dl(0), N.g1(1, 0), N.u1(0, 1), N.u0(2, 0),
-    N.m0(0, 0), N.u1(1, 0), N.m1(0, 0), N.B(2, 0), N.dl(1), N.g1(2, 0), N.u1(2, 0), N.w3(N.u),
-    N.m0(0, 1), N.w4(N.u), N.g0(1, 0), N.m1(0, 1), N.sg(0), N.g0(2, 0), N.w3(N.g), N.m0(0, 2),
-    N.w4(N.g), N.dt, N.m1(0, 2), N.m0(0, 3), N.sg(1), N.m1(0, 3), N.m0(0, 4), N.m0(1, 0),
-    N.m1(0, 4), N.m1(1, 0), N.m0(0, 5), N.m0(1, 1), N.m1(0, 5), N.m1(1, 1), N.m0(0, 6), N.m0(1, 2),
-    N.m0(2, 0), N.m1(0, 6), N.m1(1, 2), N.m1(2, 0), N.m0(0, 7), N.m0(1, 3), N.m0(2, 1), N.m0(3, 0),
-    N.m1(0, 7), N.m1(1, 3), N.m1(2, 1), N.m1(3, 0),
+    N.ex(0), N.ex(1), N.re(1), N.tn(0), N.bk(1), N.ex(2, 0), N.re(0), N.bk(0),
+    N.tn(1), N.ex(2, 1), N.ex(3, 0), N.tdf(0), N.ex(3, 1), N.dn(0), N.go(N.A, 0, 0), N.go(N.B, 0, 0),
+    N.tdf(1), N.dn(1), N.go(N.B, 0, 1), N.tdf(2), N.tdf(3), N.re(2), N.dn(2), N.go(N.A, 0, 1),
+    N.go(N.B, 0, 2), N.re(3), N.B(0, 0), N.go(N.B, 1, 0), N.bk(3), N.gg(0, 0), N.go(N.g0, 0, 0), N.gg(1, 0),
+    N.go(N.g1, 0, 0), N.uu(0, 0), N.go(N.u0, 0, 0), N.A(0, 0), N.go(N.A, 1, 0), N.uu(1, 0), N.go(N.u1, 0, 0), N.B(0, 1),
+    N.go(N.B, 1, 1), N.dn(3), N.go(N.B, 0, 3), N.bk(2), N.gg(0, 1), N.go(N.g0, 0, 1), N.gg(1, 1), N.go(N.g1, 0, 1),
+    N.B(0, 2), N.uu(0, 1), N.go(N.u0, 0, 1), N.gg(1, 2), N.gg(0, 3), N.uu(0, 2), N.uu(1, 1), N.go(N.u1, 0, 1),
+    N.uu(1, 3), N.gg(0, 2), N.uu(0, 3), N.gg(1, 3), N.fo(1), N.uu(1, 2), N.fo(3), N.B(1, 0),
+    N.go(N.B, 2, 0), N.u0(0, 0), N.go(N.u0, 1, 0), N.fo(2), N.u1(0, 0), N.go(N.u1, 1, 0), N.A(0, 1), N.go(N.A, 1, 1),
+    N.fo(0), N.mb(1), N.mb(2), N.u0(0, 1), N.go(N.u0, 1, 1), N.g0(0, 0), N.go(N.g0, 1, 0), N.B(0, 3),
+    N.g0(0, 1), N.B(1, 1), N.u1(0, 1), N.g1(0, 0), N.go(N.g1, 1, 0), N.A(1, 0), N.go(N.A, 2, 0), N.u0(1, 0),
+    N.go(N.u0, 2, 0), N.mb(3), N.mb(4), N.lo, N.mg(0, 0), N.go(N.m0, 0, 0), N.go(N.m1, 0, 0), N.go(N.m2, 0, 0),
+    N.go(N.m0, 0, 1), N.go(N.m1, 0, 1), N.go(N.m0, 0, 2), N.go(N.m2, 0, 2), N.go(N.m0, 0, 3), N.go(N.m1, 0, 4), N.go(N.m1, 0, 5), N.g1(0, 1),
+    N.mg(0, 1), N.go(N.m2, 0, 1), N.go(N.m1, 0, 2), N.go(N.m1, 0, 3), N.go(N.m2, 0, 3), N.go(N.m1, 0, 6), N.go(N.m1, 0, 7), N.mg(1, 0),
+    N.go(N.m0, 0, 4), N.go(N.m2, 0, 4), N.go(N.m0, 0, 5), N.go(N.m0, 0, 6), N.go(N.m2, 0, 6), N.go(N.m0, 0, 7), N.B(2, 0), N.dl(1),
+    N.mg(1, 1), N.go(N.m2, 0, 5), N.go(N.m2, 0, 7), N.g0(1, 0), N.go(N.g0, 2, 0), N.sg(0), N.u1(1, 0), N.go(N.u1, 2, 0),
+    N.A(1, 1), N.A(2, 0), N.m2(0, 6), N.g1(1, 0), N.go(N.g1, 2, 0), N.dl(0), N.m2(0, 0), N.go(N.m2, 1, 0),
+    N.m1(0, 0), N.go(N.m1, 1, 0), N.u0(1, 1), N.m2(0, 4), N.m1(0, 1), N.go(N.m1, 1, 1), N.sg(1), N.m2(0, 2),
+    N.go(N.m2, 1, 2), N.m2(0, 1), N.go(N.m2, 1, 1), N.m1(0, 7), N.m1(0, 4), N.m1(0, 5), N.m1(0, 2), N.go(N.m1, 1, 2),
+    N.m2(0, 5), N.m2(0, 3), N.go(N.m2, 1, 3), N.m1(0, 6), N.m2(0, 7), N.m0(0, 0), N.go(N.m0, 1, 0), N.m1(0, 3),
+    N.go(N.m1, 1, 3), N.u0(2, 0), N.m0(0, 1), N.go(N.m0, 1, 1), N.m0(0, 2), N.go(N.m0, 1, 2), N.u1(2, 0), N.m1(1, 1),
+    N.go(N.m1, 2, 1), N.w3(N.u), N.m1(1, 0), N.go(N.m1, 2, 0), N.m2(1, 0), N.go(N.m2, 2, 0), N.m2(1, 1), N.go(N.m2, 2, 1),
+    N.dt, N.m1(1, 2), N.m2(1, 3), N.g0(2, 0), N.w4(N.u), N.m0(0, 4), N.g1(2, 0), N.w3(N.g),
+    N.m2(1, 2), N.m0(1, 0), N.go(N.m0, 2, 0), N.m1(1, 3), N.m0(0, 3), N.go(N.m0, 1, 3), N.m0(0, 6), N.m2(2, 0),
+    N.go(N.m2, 3, 0), N.m2(2, 1), N.m0(0, 5), N.m0(1, 1), N.go(N.m0, 2, 1), N.m0(1, 2), N.m0(2, 0), N.go(N.m0, 3, 0),
+    N.m0(0, 7), N.m0(1, 3), N.m2(3, 0), N.m1(2, 0), N.go(N.m1, 3, 0), N.m1(2, 1), N.w4(N.g), N.m0(2, 1),
+    N.m0(3, 0), N.m1(3, 0),
 ]
 FEED = (N.ex, N.re, N.bk, N.dn, N.gg, N.uu, N.fo)
-MIXED = [N.m0, N.m1]
+EIGHTHS = {N.m0: 6, N.m1: 1, N.m2: 1}
+MIXED = list(EIGHTHS)
 DOWN = [N.A, N.B]
 GATE = [N.g0, N.g1]
 UP = [N.u0, N.u1]
@@ -266,7 +280,7 @@
     if tag in DOWN:
         return ff // rows, width // seq
     if tag in MIXED:
-        return width // rows // len(MIXED), width
+        return width // rows * EIGHTHS[tag] // 8, width
     return width // rows, ff // 4
 
 
@@ -399,7 +413,7 @@
     partners += [(row_peers[2], seq_peers[1]), (row_peers[3], seq_peers[1])]
     after = (r, lax.rem(s + 1, np.int32(4)))
     before = (r, lax.rem(s + 3, np.int32(4)))
-    first_cols, last_cols = block(1 - z1, width // 2), block(z1, width // 2)
+    df_cols = [block(2 * (z1 if w else 1 - z1) + (x if v else 1 - x), side) for w in (0, 1) for v in (0, 1)]
     active, idle = c == y, c != y
     holder, lender = c == z1, c != z1
     not_last, not_first = s < 3, s > 0
@@ -514,7 +528,6 @@
                 add(self.got.at[at], ref.at[mine])
 
             when(self.alive if p >= self.role_at else None, go)
-            self.leave(p + 1, i)
 
         def last(self):
             return At(self.got)[self.starts[-1]]
@@ -525,6 +538,9 @@
         for p in range(len(travel.order)):
             for i in range(travel.counts[p + 1]):
                 steps[tag, p, i] = functools.partial(travel.step, p, i)
+        for p in range(len(travel.order)):
+            for i in range(travel.counts[p]):
+                steps[N.go, tag, p, i] = functools.partial(travel.leave, p, i)
 
     got_tok = fetch(k.tokens.at[0], k.tok)
     got_cot = fetch(k.cotangent.at[0], k.cot)
@@ -566,11 +582,16 @@
         return k.mask[rows, i : i + 1]
 
     def gain(ref):
-        return ref[...].astype(F32)
+        return ref[...].astype(F32).reshape(1, width)
 
     step = 64
     passes = span // step
     part = span // 2
+
+    def send_df(i):
+        cols = df_cols[i]
+        src, dst = At(k.df)[pl.ds(0, span), cols], At(k.df)[pl.ds(2 * span, span), cols]
+        post(N.df_z(i), src, dst, to_z)
 
     def mixer_forward(win):
         got_win = [fetch(k.w_in.at[:, block(i, width)], win.at[:, block(i, width)]) for i in (0, 2, 1)]
@@ -594,12 +615,7 @@
             k.df[rows, :] = (mask(MASK_VALID, rows) * k.cot[rows, :].astype(F32)).astype(BF)
 
         pl.semaphore_wait(barrier, len(partners))
-        post(
-            N.df_z(0),
-            At(k.df)[pl.ds(0, span), first_cols],
-            At(k.df)[pl.ds(2 * span, span), first_cols],
-            to_z,
-        )
+        send_df(0)
         post(N.df_c, At(k.df)[pl.ds(0, span)], At(k.df)[pl.ds(span, span)], to_c)
         got_win[0].wait()
         got_win[1].wait()
@@ -669,30 +685,26 @@
         here = pl.ds(i * part, part)
         post(N.n2_z(i), At(k.n2)[here], At(k.n2)[pl.ds(2 * span + i * part, part)], to_z)
     post(N.n2_c, At(k.n2)[pl.ds(0, span)], At(k.n2)[pl.ds(span, span)], to_c)
-    post(
-        N.df_z(1),
-        At(k.df)[pl.ds(0, span), last_cols],
-        At(k.df)[pl.ds(2 * span, span), last_cols],
-        to_z,
-    )
+    for i in (1, 2, 3):
+        send_df(i)
     post(N.nrm_c, At(k.nrm)[pl.ds(0, span)], At(k.nrm)[pl.ds(span, span)], to_c)
     post(N.gat_c, At(k.gat)[pl.ds(0, span)], At(k.gat)[pl.ds(span, span)], to_c)
 
     z_rows, t_rows = pl.ds(2 * span, span), pl.ds(3 * span, span)
     z_parts = [pl.ds(2 * span + i * part, part) for i in range(2)]
     t_parts = [pl.ds(3 * span + i * part, part) for i in range(2)]
-    half_cols = (first_cols, last_cols)
 
     def pass_df(i):
-        arrived(N.df_z(i), At(k.df)[z_rows, half_cols[i]])
-        post(N.df_t(i), At(k.df)[z_rows, half_cols[i]], At(k.df)[t_rows, half_cols[i]], to_c)
+        arrived(N.df_z(i), At(k.df)[z_rows, df_cols[i]])
+        post(N.df_t(i), At(k.df)[z_rows, df_cols[i]], At(k.df)[t_rows, df_cols[i]], to_c)
 
     def pass_n2(i):
         arrived(N.n2_z(i), At(k.n2)[z_parts[i]])
         post(N.n2_t(i), At(k.n2)[z_parts[i]], At(k.n2)[t_parts[i]], to_c)
 
+    for i in range(4):
+        steps[N.tdf(i)] = functools.partial(pass_df, i)
     for i in range(2):
-        steps[N.tdf(i)] = functools.partial(pass_df, i)
         steps[N.tn(i)] = functools.partial(pass_n2, i)
 
     def down_last(i):
@@ -816,6 +828,12 @@
 
         own = steps
 
+        waiting = [got_wd]
+
+        def take_wd():
+            while waiting:
+                waiting.pop().wait()
+
         def ex0():
             got_wg.wait()
             got_wu.wait()
@@ -826,10 +844,11 @@
             expand(pl.ds(span, span), False)
 
         def re0():
-            got_wd.wait()
+            take_wd()
             retreat(0, False)
 
         def re1():
+            take_wd()
             arrived(N.df_c, At(k.df)[pl.ds(span, span)])
             retreat(1, False)
 
@@ -862,7 +881,6 @@
             rel = unit_bits(tag, u)
             rho = 4 * chosen(rel[N.y], y) + 2 * chosen(rel[N.x], x) + core
             travel.own[u] = dot_tn(k.n2[:, block(rho, slim)], grad[...]).astype(BF)
-            travel.leave(0, u)
 
         def to_ref(ref, plus=None):
             def store(cols, value):
@@ -901,35 +919,28 @@
         own.update({N.fo(0): fo0, N.fo(1): fo1, N.fo(2): fo2, N.fo(3): fo3})
         own[N.re(2)] = functools.partial(retreat, 2, True)
 
+        taken_df = set()
+
+        def take_df(i):
+            if i not in taken_df:
+                taken_df.add(i)
+                arrived(N.df_t(i), At(k.df)[t_rows, df_cols[i]])
+
         def re3():
-            arrived_df1()
+            for i in range(4):
+                take_df(i)
             retreat(3, True)
 
-        seen = []
-
-        def arrived_df1():
-            if not seen:
-                seen.append(1)
-                arrived(N.df_t(1), At(k.df)[t_rows, half_cols[1]])
-
-        def dn1():
-            arrived_df1()
-            grads_down(1)
-
-        def dn0():
-            arrived(N.df_t(0), At(k.df)[t_rows, half_cols[0]])
-            grads_down(0)
-
-        def grads_down(rel_w):
-            for rel_x in range(2):
-                sigma = 2 * chosen(rel_w, z1) + chosen(rel_x, x)
-                value = dot_tn(hid[...], k.df[:, block(sigma, side)])
-                for i, tag in enumerate(DOWN):
-                    u = unit_index(tag, {N.x: rel_x, N.z1: rel_w})
-                    travels[tag].own[u] = value[i * tall : (i + 1) * tall].astype(BF)
-                    travels[tag].leave(0, u)
-
-        own.update({N.re(3): re3, N.dn(0): dn0, N.dn(1): dn1})
+        def dn(i):
+            take_df(i)
+            rel = {N.x: i % 2, N.z1: i // 2}
+            value = dot_tn(hid[...], k.df[:, df_cols[i]])
+            for j, tag in enumerate(DOWN):
+                travels[tag].own[unit_index(tag, rel)] = value[j * tall : (j + 1) * tall].astype(BF)
+
+        own[N.re(3)] = re3
+        for i in range(4):
+            own[N.dn(i)] = functools.partial(dn, i)
         for i in range(2):
             own[N.ex(2, i)] = functools.partial(ex2, i)
             own[N.ex(3, i)] = functools.partial(ex3, i)
@@ -949,11 +960,16 @@
         pltpu.VMEM((4 * span, quarter), BF),
     )
 
-    def mixer_backward(win, gm):
+    shares, start = {}, 0
+    for tag in MIXED:
+        size = unit_shape(tag, slim * 8, 0, 8, 4)[0]
+        shares[tag] = slice(start, start + size)
+        start += size
+
+    def mixer_backward(win, *own_mixed):
         got_win = fetch(k.w_in, win)
-        share = slim // len(MIXED)
-        for h, tag in enumerate(MIXED):
-            travels[tag].own = gm.at[h]
+        for tag, own in zip(MIXED, own_mixed):
+            travels[tag].own = own
 
         def mb1():
             arrived(N.pz, k.pz)
@@ -1056,31 +1072,21 @@
         def mg(rel_x, rel_y):
             rho = 4 * chosen(rel_y, y) + 2 * chosen(rel_x, x) + c
             rows = block(rho, slim)
-            leaving = []
             for a in range(2):
                 for b in range(2):
                     sigma = 2 * chosen(b, z1) + chosen(a, z0)
                     first = dot_tn(k.nrm[:, rows], k.dpj[:, block(sigma, wide)])
                     second = dot_tn(k.gat[:, rows], k.dmx[:, block(sigma, side)])
-                    for h, tag in enumerate(MIXED):
+                    for tag in MIXED:
                         u = unit_index(tag, {N.x: rel_x, N.y: rel_y, N.z0: a, N.z1: b})
-                        here = slice(h * share, (h + 1) * share)
-                        gm[h, u, :, :wide] = first[here].astype(BF)
-                        gm[h, u, :, wide:] = second[here].astype(BF)
-                        leaving.append((u, tag, h))
-            for u, tag, h in sorted(leaving):
-                leave_mixed(tag, h, u)
-
-        def leave_mixed(tag, h, u):
-            travel = travels[tag]
-            if u < travel.counts[0] // 2:
-                dst = At(travel.got)[travel.starts[0] + u]
-                post((tag, 0, u), At(gm)[h, u], dst, to_dim[travel.order[0]])
+                        own = travels[tag].own
+                        own[u, :, :wide] = first[shares[tag]].astype(BF)
+                        own[u, :, wide:] = second[shares[tag]].astype(BF)
 
         def finish_mixed():
-            for h, tag in enumerate(MIXED):
+            for tag in MIXED:
                 got, at = travels[tag].got, travels[tag].starts[-1]
-                rows = pl.ds(h * share, share)
+                rows = pl.ds(shares[tag].start, shares[tag].stop - shares[tag].start)
                 put(At(got)[at, :, pl.ds(0, wide)], At(k.g_in)[rows, :])
                 put(At(got)[at, :, pl.ds(wide, width - wide)], At(k.g_out)[rows, :])
 
@@ -1099,7 +1105,7 @@
     pl.run_scoped(
         mixer_backward,
         pltpu.VMEM((width, 3 * width), BF),
-        pltpu.VMEM((len(MIXED), 16, slim // len(MIXED), width), BF),
+        *[pltpu.VMEM((16, shares[tag].stop - shares[tag].start, width), BF) for tag in MIXED],
     )
 
 
@@ -1184,9 +1190,9 @@
         valid_counts,
         tokens,
         cotangent,
-        norm_in[None],
+        norm_in,
         w_conv,
-        norm_ffn[None],
+        norm_ffn,
         w_in,
         w_out,
         w_gate,

time: 152 us -> 143 us (0.941)
  Pallas kernels: 147 us -> 142 us
  local copies, waits for them, and re-layouts: 2.56 us -> 0 us
    pallas_call x1, Pallas kernels: 143 us -> 137 us  [fused(): pl.pallas_call(functools.partial(layer_kernel, OPERANDS + list(scratch)),...]
    broadcast_in_dim x2 -> x0, local copies, waits for them, and re-layouts: 2.56 us -> none  [the longest x1 1.28 us: fused(): norm_in[None]]
where the time goes in v3:
time: 143 us
  Pallas kernels  142 us (99%)
  between operations  1.48 us (1%)
    pallas_call x1, Pallas kernels, fused(): pl.pallas_call(functools.partial(layer_kernel, OPERANDS + list(scratch)),...  137 us
    pallas_call x1, Pallas kernels, fused(): pl.pallas_call(functools.partial(finish_kernel, n), out_shape=[jax.ShapeD...  4.15 us

profile of v3, /device:TPU:0, one launch (start us, length us, event | category | flops | bytes accessed | tf_op | source)
XLA Modules:
  0.0 143.0 jit_solution(9734037315691832679)
XLA Ops:
  1.3 137.4 %layer.1 = (bf16[1,256,1024]{2,1,0:T(8,128)(2,1)}, bf16[1,256,1024]{2,1,0:T(8,128)(2,1)}, bf16[128,768]{1,0:T(8,128)(2,1)}, bf16[128,256]{1,0:T(8,128)(2,1)}, bf...) custom-call(s32[1,8]{1,0:T(1,128)} %refs_0_.1, ...), custom_call_target="tpu_custom_call" | custom-call | tf_op jit(solution)/shard_map/layer/pallas_call | solution.py:1176
  138.7 4.1 %finish.1 = (bf16[1,256,1024]{2,1,0:T(8,128)(2,1)}, bf16[1,256,1024]{2,1,0:T(8,128)(2,1)}, f32[128,768]{1,0:T(8,128)}, f32[128,256]{1,0:T(8,128)}, f32[128,1152]...) custom-call(bf16[1,256,1024]{2,1,0:T(8,128)(2,1)} %get-tuple-element, ...), custom_call_target="tpu_custom_call" | custom-call | tf_op jit(solution)/shard_map/finish/pallas_call | solution.py:1205
